TPU v7x, 32 devices: a whole 2x2x4 slice. The times are simulated.
32 devices in a mesh: mode: 16 (over z, x, core), mesh: 2 (over y).
Axes of the slice: x: 2, y: 2, z: 4, core: 2. Of those that a mesh axis runs over, the one named last changes fastest.
Arguments:
- velocity: float32 [3, 11, 11, 2, 32, 512], P(None, None, None, 'mesh', 'mode'), may hold values from -6 to 6
- penalty: float32 [11, 11, 2, 32], P(None, None, 'mesh'), may hold values from 0.5 to 8
Outputs:
- solution: float32 [512, 3, 11, 11, 2, 32], P('mode', None, None, None, 'mesh')
All inputs are finite; a program needn't handle non-finite values.
Results may differ from a plain program's by a relative error of at most 0.0001.
Values sent between devices are 32-bit elements; how exact they have to be, the bound alone decides.
No kernel may reach another device: no remote copies, remote signals or barrier semaphores. Data moves between devices by JAX's collectives and lax.ppermute only.
A program may use at most 256 MiB of HBM per device.

v0:
```python
import math

import jax
import jax.numpy as jnp
import numpy as np
from jax import lax
from jax.sharding import PartitionSpec as P

ORDER = 10
PLANES = 512
MODES = 256
ITERS = 6


helm_base = 1.0
span_wave = 0.02
bound_ratio = 25.0


def legendre_pair(points, order):
    previous = points * 0.0 + 1.0
    current = points * 1.0
    for degree in range(2, order + 1):
        following = ((2 * degree - 1) * points * current - (degree - 1) * previous) / degree
        previous = current
        current = following
    return (current, previous)


def gll_tables(order):
    count = order + 1
    points = -np.cos(np.pi * np.arange(count) / order)
    for sweep in range(200):
        top_vals, below_vals = legendre_pair(points, order)
        points = points - (points * top_vals - below_vals) / (count * top_vals)
    legendre_vals, below_vals = legendre_pair(points, order)
    weights = 2.0 / (order * (order + 1) * legendre_vals**2)
    identity = np.eye(count)
    spacing = points[:, None] - points[None, :] + identity
    derivative = legendre_vals[:, None] / (legendre_vals[None, :] * spacing) * (1.0 - identity)
    corner = np.concatenate(
        [[-order * (order + 1) / 4.0], np.zeros(order - 1), [order * (order + 1) / 4.0]]
    )
    derivative = derivative + identity * corner[None, :]
    stiffness = derivative.T @ (weights[:, None] * derivative)
    weight_mat = identity * weights[None, :]
    laplace = np.kron(stiffness, weight_mat) + np.kron(weight_mat, stiffness)
    upper_bound = float(
        np.max(np.sum(np.abs(laplace), axis=1) / np.sum(laplace * np.eye(count * count), axis=1))
    )
    weight_vec = jnp.asarray(weights, jnp.float32)
    stiff_mat = jnp.asarray(stiffness, jnp.float32)
    deriv_mat = jnp.asarray(derivative, jnp.float32)
    mass_two = weight_vec[:, None] * weight_vec[None, :]
    stiff_diag = jnp.diagonal(stiff_mat)
    lap_diag = stiff_diag[:, None] * weight_vec[None, :] + weight_vec[:, None] * stiff_diag[None, :]
    return (weight_vec, stiff_mat, deriv_mat, mass_two, lap_diag, upper_bound)


def dft_table(planes, modes):
    plane_index = jnp.arange(planes, dtype=jnp.int32)
    mode_index = jnp.arange(modes, dtype=jnp.int32)
    phase_turns = plane_index[:, None] * mode_index[None, :] % planes
    angles = 2.0 * math.pi / planes * phase_turns.astype(jnp.float32)
    return jnp.concatenate([jnp.cos(angles), -jnp.sin(angles)], axis=1) / math.sqrt(planes)


def advect(along_first, along_second, field, deriv_mat):
    grad_first = jnp.einsum(
        "ia,...abxyz->...ibxyz", deriv_mat, field, precision=lax.Precision.HIGHEST
    )
    grad_second = jnp.einsum(
        "jb,...abxyz->...ajxyz", deriv_mat, field, precision=lax.Precision.HIGHEST
    )
    return field - (along_first * grad_first + along_second * grad_second)


def make_coeff(first_row, count, penalty, mass_two):
    rows = (first_row + jnp.arange(count, dtype=jnp.int32)).astype(jnp.int32)
    wave = (rows % MODES).astype(jnp.float32)
    helm = helm_base + (span_wave * wave) ** 2
    return (helm[:, None, None, None, None, None] + penalty[None, None]) * mass_two[
        None, None, :, :, None, None
    ]


def assemble(field, neighbours):
    top = field[:, :, :, -1]
    bottom = field[:, :, :, 0]
    shared = top[..., :-1] + bottom[..., 1:]
    top_new = jnp.concatenate([shared, top[..., -1:]], axis=-1)
    bottom_new = jnp.concatenate([bottom[..., :1], shared], axis=-1)
    field = field.at[:, :, :, -1].set(top_new).at[:, :, :, 0].set(bottom_new)
    right = field[:, :, -1]
    left = field[:, :, 0]
    shared = right[:, :, :, :-1] + left[:, :, :, 1:]
    from_lower, from_upper = neighbours(right[:, :, :, -1], left[:, :, :, 0])
    right_new = jnp.concatenate([shared, (right[:, :, :, -1] + from_upper)[:, :, :, None]], axis=3)
    left_new = jnp.concatenate([(left[:, :, :, 0] + from_lower)[:, :, :, None], shared], axis=3)
    return field.at[:, :, -1].set(right_new).at[:, :, 0].set(left_new)


def no_neighbours(right_edge, left_edge):
    return (jnp.zeros_like(right_edge), jnp.zeros_like(left_edge))


def helm_apply(field, coeff, stiff_mat, weight_vec):
    along_first = jnp.einsum("ia,rcabxy->rcibxy", stiff_mat, field, precision=lax.Precision.HIGHEST)
    along_second = jnp.einsum(
        "jb,rcabxy->rcajxy", stiff_mat, field, precision=lax.Precision.HIGHEST
    )
    along_first = along_first * weight_vec[None, None, None, :, None, None]
    along_second = along_second * weight_vec[None, None, :, None, None, None]
    return along_first + along_second + coeff * field


def chebyshev(spectra, coeff, tables, neighbours):
    weight_vec, stiff_mat, deriv_mat, mass_two, lap_diag, upper_bound = tables
    lower_bound = upper_bound / bound_ratio
    midpoint = (upper_bound + lower_bound) / 2.0
    half_width = (upper_bound - lower_bound) / 2.0
    rhs = assemble(mass_two[None, None, :, :, None, None] * spectra, neighbours)
    diagonal = assemble(lap_diag[None, None, :, :, None, None] + coeff, neighbours)
    inverse = 1.0 / diagonal
    iterate = jnp.zeros_like(rhs)
    residual = rhs
    direction = inverse * residual / midpoint
    recurrence = half_width / midpoint
    for step in range(ITERS):
        iterate = iterate + direction
        residual = residual - assemble(
            helm_apply(direction, coeff, stiff_mat, weight_vec), neighbours
        )
        if step + 1 < ITERS:
            recurrence_next = 1.0 / (2.0 * midpoint / half_width - recurrence)
            direction = (
                recurrence_next * recurrence * direction
                + 2.0 * recurrence_next / half_width * inverse * residual
            )
            recurrence = recurrence_next
    return iterate


def per_device(velocity, penalty):
    tables = gll_tables(ORDER)
    forcing = advect(velocity[0], velocity[1], velocity, tables[2])
    table = dft_table(PLANES, MODES)
    spectra = jnp.einsum("cabxyz,zk->kcabxy", forcing, table, precision=lax.Precision.HIGHEST)
    owned = lax.all_to_all(
        lax.all_to_all(spectra, "mode", split_axis=0, concat_axis=5, tiled=True),
        "mesh",
        split_axis=0,
        concat_axis=4,
        tiled=True,
    )
    full_penalty = lax.all_gather(penalty, "mesh", axis=2, tiled=True)
    row_count = owned.shape[0]
    first_row = (
        lax.axis_index("mode") * lax.axis_size("mesh") + lax.axis_index("mesh")
    ) * row_count
    coeff = make_coeff(first_row, row_count, full_penalty, tables[3])
    solved = chebyshev(owned, coeff, tables, no_neighbours)
    return lax.all_to_all(solved, "mesh", split_axis=4, concat_axis=0, tiled=True)


def solution(mesh):
    return jax.shard_map(
        per_device,
        mesh=mesh,
        in_specs=(P(None, None, None, "mesh", "mode", None), P(None, None, "mesh", None)),
        out_specs=P("mode", None, None, None, "mesh", None),
        check_vma=False,
    )
```

profile of v0, /device:TPU:0, one launch (start us, length us, event | category | flops | bytes accessed | tf_op | source)
XLA Modules:
  0.0 585.1 jit_solution(731724230706500464)
XLA Ops:
  6.5 3.0 fusion.31
  9.5 4.1 fusion.38
  13.7 18.8 %copy.279 = f32[512,3,11,11,1,2]{3,5,2,1,4,0:T(2,128)} copy(f32[512,3,11,11,1,2]{0,3,5,2,1,4:T(8,128)S(1)} %fusion.38) | data formatting | bytes 2973696 | tf_op jit(solution)/shard_map/cabxyz,zk->kcabxy/dot_general | solution.py:148
  32.5 27.0 %reshape.1407 = f32[16,1,23232]{2,1,0:T(1,128)} reshape(f32[512,1,3,11,2,11]{5,4,3,2,1,0:T(2,128)} %bitcast.335) | data formatting | bytes 2973696
  59.5 7.4 %all-to-all-start = ((f32[16,1,23232]{2,1,0:T(1,128)}), f32[16,1,23232]{2,1,0:T(1,128)S(1)}, u32[]{:S(2)}, u32[]{:S(2)}) async-start(f32[16,1,23232]{2,1,0:T(1,128)} %reshape.1407), calls=%async_computation | async-start | bytes 2981888 | tf_op jit(solution)/shard_map/all_to_all | solution.py:150
  67.9 5.6 all_gather.3
  79.8 17.6 %all-to-all-done = f32[16,1,23232]{2,1,0:T(1,128)S(1)} async-done(((f32[16,1,23232]{2,1,0:T(1,128)}), f32[16,1,23232]{2,1,0:T(1,128)S(1)}, u32[]{:S(2)}, u32[]{:S(2)}) %all-to-all-start) | async-done | bytes 1486880 | tf_op jit(solution)/shard_map/all_to_all | solution.py:150
  97.8 5.6 reduce.56
  103.4 36.7 %reshape.1408 = f32[512,1,3,11,2,11]{5,4,3,2,1,0:T(2,128)} reshape(f32[16,23232]{1,0:T(8,128)} %reduce.56) | data formatting | bytes 2973696
  140.1 24.9 %copy.351 = f32[16,32,3,11,11,1,2]{1,0,6,4,3,2,5:T(8,128)} copy(f32[16,32,3,11,11,1,2]{4,6,3,2,1,0,5:T(2,128)} %bitcast.336) | data formatting | bytes 2973696 | tf_op jit(solution)/shard_map/all_to_all | solution.py:150
  165.0 8.4 %copy.281 = f32[32,3,11,11,1,16,2]{0,6,5,3,2,1,4:T(2,128)} copy(f32[32,3,11,11,1,16,2]{0,5,6,3,2,1,4:T(8,128)} %bitcast.340) | data formatting | bytes 2973696 | tf_op jit(solution)/shard_map/all_to_all | solution.py:150
  173.4 7.1 %reduce.57 = f32[32,3,11,11,32]{0,4,3,2,1:T(8,128)} reduce(f32[32,3,11,11,1,32]{0,5,3,2,1,4:T(8,128)} %bitcast.341, f32[]{:T(128)} %broadcast.552), dimensions={4}, to_apply=%copy.282.reduce_sub_computation | reduce | bytes 2973700 | tf_op jit(solution)/shard_map/all_to_all | solution.py:150
  180.5 10.4 %copy.465 = f32[32,3,11,11,32]{4,3,2,1,0:T(8,128)} copy(f32[32,3,11,11,32]{0,4,3,2,1:T(8,128)} %reduce.57) | data formatting | bytes 2973696
  190.9 9.3 %reshape.1409 = f32[2,1,185856]{2,1,0:T(1,128)} reshape(f32[32,3,11,11,32]{4,3,2,1,0:T(8,128)} %copy.465) | data formatting | bytes 2973696
  200.1 3.7 all-to-all-start.1
  207.0 6.3 %multiply_bitcast_fusion = (f32[16,11,11,2,32]{4,0,2,3,1:T(8,128)}, f32[16,11,11,2,32]{4,0,2,3,1:T(8,128)}, f32[16,11,11,2,32]{4,0,2,3,1:T(8,128)}, f32[16,11,11...) fusion(f32[16,1,11,11,2,32]{5,0,3,4,2,1:T(8,128)} %fusion.82), kind=kLoop, calls=%fused_computation.65 | loop fusion | flops 743424 | bytes 3469312 | tf_op jit(solution)/shard_map/mul | solution.py:138
  213.3 10.2 %all-to-all-done.1 = f32[2,1,185856]{2,1,0:T(1,128)S(1)} async-done(((f32[2,1,185856]{2,1,0:T(1,128)}), f32[2,1,185856]{2,1,0:T(1,128)S(1)}, u32[]{:S(2)}, u32[]{:S(2)}) %all-to-all-start.1) | async-done | bytes 1486880 | tf_op jit(solution)/shard_map/all_to_all | solution.py:149
  223.5 6.3 %reduce.58 = f32[2,185856]{1,0:T(2,128)} reduce(f32[2,1,185856]{2,1,0:T(1,128)S(1)} %all-to-all-done.1, f32[]{:T(128)} %broadcast.552), dimensions={1}, to_apply=%all_to_all.43.reduce_sub_computation | reduce | bytes 2973700 | tf_op jit(solution)/shard_map/all_to_all | solution.py:149
  229.8 15.4 %reshape.1410 = f32[32,3,11,11,1,32]{5,4,3,2,1,0:T(1,128)} reshape(f32[2,185856]{1,0:T(2,128)} %reduce.58) | data formatting | bytes 2973696
  245.2 3.5 copy.283
  253.7 13.1 %fusion.16 = f32[16,3,11,2,32,11]{4,5,3,2,1,0:T(8,128)S(1)} fusion(f32[11,11,1,1,1,1]{1,0,5,4,3,2:T(8,128)S(1)} %copy-done.13, f32[16,3,11,11,2,32]{5,0,4,1,2,3:T(8,128)S(1)} %multiply_multiply_fusion), kind=kOutput, calls=%fused_computation.17 | convolution fusion | flops 49065984 | bytes 2974180 | tf_op jit(solution)/shard_map/jb,rcabxy->rcajxy/dot_general | solution.py:109
  266.8 14.2 %fusion.18 = f32[16,3,11,2,32,11]{4,5,3,2,1,0:T(8,128)} fusion(f32[11,11,1,1,1,1]{1,0,5,4,3,2:T(8,128)S(1)} %copy-done.13, f32[16,3,11,11,2,32]{5,0,4,1,2,3:T(8,128)S(1)} %multiply_multiply_fusion), kind=kOutput, calls=%fused_computation.19 | convolution fusion | flops 49065984 | bytes 2974180 | tf_op jit(solution)/shard_map/ia,rcabxy->rcibxy/dot_general | solution.py:108
  281.0 10.5 %fusion.24 = f32[16,3,11,11,2,32]{5,0,4,1,2,3:T(8,128)} fusion(f32[16,3,11,2,32,11]{4,5,3,2,1,0:T(8,128)S(1)} %fusion.16, f32[16,3,11,2,32,11]{4,5,3,2,1,0:T(8,128)} %fusion.18, f32[16,3,11,11,2,32]{5,0,4,1,2,3:T(8,128)S(1)} %fusion.50, f32[11]{0:T(128)S(1)} %copy-done.14, f32[16,11,11,2,32]{4,0,2,3,1:T(8,128)} %get-tuple-element.403, ...), kind=kLoop, calls=%fused_computation.31 | loop fusion | flops 2230272 | bytes 6938668 | tf_op jit(solution)/shard_map/add | solution.py:114
  298.3 7.4 %fusion.92 = (f32[16,3,11,11,2,32]{5,0,4,1,2,3:T(8,128)}, f32[16,3,11,11,2,32]{5,0,4,1,2,3:T(8,128)S(1)}, f32[16,3,11,11,2,32]{5,0,4,1,2,3:T(8,128)}) fusion(f32[16,3,11,11,2,32]{5,0,4,1,2,3:T(8,128)S(1)} %fusion.50, f32[16,3,11,11,2,32]{5,0,4,1,2,3:T(8,128)} %fusion.54, f32[16,11,11,2,32]{4,0,2,3,1:T(8,128)S(1)} %copy-done.5, ...), kind=kLoop, calls=%fused_computation.206 | loop fusion | flops 2601984 | bytes 8425472 | tf_op jit(solution)/shard_map/add | solution.py:130
  305.7 14.3 %fusion.14 = f32[16,3,11,2,32,11]{4,5,3,2,1,0:T(8,128)} fusion(f32[11,11,1,1,1,1]{1,0,5,4,3,2:T(8,128)S(1)} %copy-done.13, f32[16,3,11,11,2,32]{5,0,4,1,2,3:T(8,128)S(1)} %get-tuple-element.342), kind=kOutput, calls=%fused_computation.15 | convolution fusion | flops 49065984 | bytes 2974180 | tf_op jit(solution)/shard_map/ia,rcabxy->rcibxy/dot_general | solution.py:108
  320.1 14.2 %fusion.12 = f32[16,3,11,2,32,11]{4,5,3,2,1,0:T(8,128)} fusion(f32[11,11,1,1,1,1]{1,0,5,4,3,2:T(8,128)S(1)} %copy-done.13, f32[16,3,11,11,2,32]{5,0,4,1,2,3:T(8,128)S(1)} %get-tuple-element.342), kind=kOutput, calls=%fused_computation.13 | convolution fusion | flops 49065984 | bytes 2974180 | tf_op jit(solution)/shard_map/jb,rcabxy->rcajxy/dot_general | solution.py:109
  334.2 12.6 %fusion.23 = (f32[16,3,11,11,2,32]{5,0,4,1,2,3:T(8,128)S(1)}, f32[16,3,11,11,2,32]{5,0,4,1,2,3:T(8,128)}) fusion(f32[16,3,11,2,32,11]{4,5,3,2,1,0:T(8,128)} %fusion.12, f32[16,3,11,2,32,11]{4,5,3,2,1,0:T(8,128)} %fusion.14, f32[16,3,11,11,2,32]{5,0,4,1,2,3:T(8,128)S(1)} %get-tuple-element.342, f32[11]{0:T(128)S(1)} %copy-done.14, ...), kind=kLoop, calls=%fused_computation.29 | loop fusion | flops 2230272 | bytes 7929900 | tf_op jit(solution)/shard_map/add | solution.py:114
  348.4 2.9 copy.308
  352.2 10.9 %copy_add_fusion.1 = f32[16,3,11,11,2,32]{5,0,3,4,2,1:T(8,128)} fusion(f32[16,3,11,11,2,32]{5,0,4,1,2,3:T(8,128)} %get-tuple-element.363, f32[16,11,11,2,32]{4,0,2,3,1:T(8,128)} %get-tuple-element.374, f32[16,3,11,11,2,32]{5,0,3,4,2,1:T(8,128)} %fusion.58, f32[16,3,11,11,2,32]{5,0,4,1,2,3:T(8,128)} %get-tuple-element.343), kind=kLoop, calls=%fused_computation.42 | loop fusion | flops 1115136 | bytes 6443008 | tf_op jit(solution)/shard_map/add | solution.py:137
  363.1 14.2 %fusion.8 = f32[16,3,11,2,32,11]{4,5,3,2,1,0:T(8,128)} fusion(f32[11,11,1,1,1,1]{1,0,5,4,3,2:T(8,128)S(1)} %copy-done.13, f32[16,3,11,11,2,32]{5,0,3,4,2,1:T(8,128)} %copy_add_fusion.1), kind=kOutput, calls=%fused_computation.9 | convolution fusion | flops 49065984 | bytes 2974180 | tf_op jit(solution)/shard_map/jb,rcabxy->rcajxy/dot_general | solution.py:109
  377.3 14.5 %fusion.10 = f32[16,3,11,2,32,11]{4,5,3,2,1,0:T(8,128)} fusion(f32[11,11,1,1,1,1]{1,0,5,4,3,2:T(8,128)S(1)} %copy-done.13, f32[16,3,11,11,2,32]{5,0,3,4,2,1:T(8,128)S(1)} %copy-done), kind=kOutput, calls=%fused_computation.11 | convolution fusion | flops 49065984 | bytes 2974180 | tf_op jit(solution)/shard_map/ia,rcabxy->rcibxy/dot_general | solution.py:108
  391.9 10.0 %fusion.22 = f32[16,3,11,11,2,32]{5,0,3,4,2,1:T(8,128)S(1)} fusion(f32[16,3,11,2,32,11]{4,5,3,2,1,0:T(8,128)} %fusion.8, f32[16,3,11,2,32,11]{4,5,3,2,1,0:T(8,128)} %fusion.10, f32[16,3,11,11,2,32]{5,0,3,4,2,1:T(8,128)S(1)} %copy-done, f32[11]{0:T(128)S(1)} %copy-done.14, f32[16,11,11,2,32]{4,0,2,3,1:T(8,128)S(1)} %get-tuple-element.402), kind=kLoop, calls=%fused_computation.27 | loop fusion | flops 1858560 | bytes 6443052 | tf_op jit(solution)/shard_map/add | solution.py:114
  403.2 3.0 copy-done.2
  407.6 5.5 multiply_add_fusion.1
  413.1 14.7 %fusion.4 = f32[16,3,11,2,32,11]{4,5,3,2,1,0:T(8,128)} fusion(f32[11,11,1,1,1,1]{1,0,5,4,3,2:T(8,128)S(1)} %copy-done.13, f32[16,3,11,11,2,32]{5,0,3,4,2,1:T(8,128)S(1)} %multiply_add_fusion.1), kind=kOutput, calls=%fused_computation.5 | convolution fusion | flops 49065984 | bytes 2974180 | tf_op jit(solution)/shard_map/jb,rcabxy->rcajxy/dot_general | solution.py:109
  427.8 14.3 %fusion.6 = f32[16,3,11,2,32,11]{4,5,3,2,1,0:T(8,128)} fusion(f32[11,11,1,1,1,1]{1,0,5,4,3,2:T(8,128)S(1)} %copy-done.13, f32[16,3,11,11,2,32]{5,0,3,4,2,1:T(8,128)S(1)} %multiply_add_fusion.1), kind=kOutput, calls=%fused_computation.7 | convolution fusion | flops 49065984 | bytes 2974180 | tf_op jit(solution)/shard_map/ia,rcabxy->rcibxy/dot_general | solution.py:108
  442.1 12.4 %fusion.21 = f32[16,3,11,11,2,32]{5,0,3,4,2,1:T(8,128)} fusion(f32[16,3,11,2,32,11]{4,5,3,2,1,0:T(8,128)} %fusion.4, f32[16,3,11,2,32,11]{4,5,3,2,1,0:T(8,128)} %fusion.6, f32[16,3,11,11,2,32]{5,0,3,4,2,1:T(8,128)S(1)} %multiply_add_fusion.1, f32[11]{0:T(128)S(1)} %copy-done.14, f32[16,11,11,2,32]{4,0,2,3,1:T(8,128)S(1)} %get-tuple-element.402), kind=kLoop, calls=%fused_computation.25 | loop fusion | flops 1858560 | bytes 6443052 | tf_op jit(solution)/shard_map/add | solution.py:114
  461.5 15.4 %multiply_add_fusion = (f32[16,3,11,11,2,32]{5,0,3,4,2,1:T(8,128)}, f32[16,3,11,11,2,32]{5,0,3,4,2,1:T(8,128)}) fusion(f32[16,3,11,11,2,32]{5,0,3,4,2,1:T(8,128)} %copy-done.1, f32[16,11,11,2,32]{4,0,2,3,1:T(8,128)S(1)} %copy-done.8, f32[16,3,11,11,2,32]{5,0,3,4,2,1:T(8,128)} %fusion.66, f32[16,3,11,11,2,32]{5,0,3,4,2,1:T(8,128)} %copy-done.2, ...), kind=kLoop, calls=%fused_computation.48 | loop fusion | flops 2230272 | bytes 10903552 | tf_op jit(solution)/shard_map/add | solution.py:137
  476.9 14.2 %fusion = f32[16,3,11,2,32,11]{4,5,3,2,1,0:T(8,128)} fusion(f32[11,11,1,1,1,1]{1,0,5,4,3,2:T(8,128)S(1)} %copy-done.13, f32[16,3,11,11,2,32]{5,0,3,4,2,1:T(8,128)} %get-tuple-element.344), kind=kOutput, calls=%fused_computation.1 | convolution fusion | flops 49065984 | bytes 2974180 | tf_op jit(solution)/shard_map/jb,rcabxy->rcajxy/dot_general | solution.py:109
  491.1 14.4 %fusion.2 = f32[16,3,11,2,32,11]{4,5,3,2,1,0:T(8,128)} fusion(f32[11,11,1,1,1,1]{1,0,5,4,3,2:T(8,128)S(1)} %copy-done.13, f32[16,3,11,11,2,32]{5,0,3,4,2,1:T(8,128)S(1)} %bitcast.332), kind=kOutput, calls=%fused_computation.3 | convolution fusion | flops 49065984 | bytes 2974180 | tf_op jit(solution)/shard_map/ia,rcabxy->rcibxy/dot_general | solution.py:108
  505.6 11.9 %fusion.20 = f32[16,3,11,11,2,32]{5,0,3,4,2,1:T(8,128)} fusion(f32[16,3,11,2,32,11]{4,5,3,2,1,0:T(8,128)} %fusion, f32[16,3,11,2,32,11]{4,5,3,2,1,0:T(8,128)} %fusion.2, f32[16,3,11,11,2,32]{5,0,3,4,2,1:T(8,128)S(1)} %bitcast.332, f32[11]{0:T(128)S(1)} %copy-done.14, f32[16,11,11,2,32]{4,0,2,3,1:T(8,128)S(1)} %get-tuple-element.402), kind=kLoop, calls=%fused_computation.23 | loop fusion | flops 1858560 | bytes 6443052 | tf_op jit(solution)/shard_map/add | solution.py:114
  524.5 13.7 %copy_bitcast_fusion = f32[2,3,11,11,16,32]{5,4,3,2,1,0:T(8,128)} fusion(f32[16,3,11,11,2,32]{5,0,3,4,2,1:T(8,128)} %get-tuple-element.344, f32[16,3,11,11,2,32]{5,0,3,4,2,1:T(8,128)} %copy-done.1, f32[16,3,11,11,2,32]{5,0,3,4,2,1:T(8,128)S(1)} %copy-done, f32[16,3,11,11,2,32]{5,0,4,1,2,3:T(8,128)} %get-tuple-element.341, ...), kind=kLoop, calls=%fused_computation.214 | loop fusion | flops 2973696 | bytes 10903552
  538.2 4.7 reshape.1411
  542.9 21.3 %all_to_all.54 = f32[2,1,185856]{2,1,0:T(1,128)S(1)} all-to-all(f32[2,1,185856]{2,1,0:T(1,128)S(1)} %reshape.1411), channel_id=1, replica_groups=mesh['mode'=16,'mesh'=2] {'mesh'}, dimensions={0} | all-to-all | bytes 2973696 | tf_op jit(solution)/shard_map/all_to_all | solution.py:163
  564.2 4.9 reduce.59
  569.1 5.0 reshape.1412
  574.1 3.6 copy.346
  577.7 7.2 %copy.347 = f32[32,3,11,11,1,32]{5,4,3,2,1,0:T(1,128)} copy(f32[32,3,11,11,1,32]{5,0,3,2,1,4:T(8,128)S(1)} %bitcast.343) | data formatting | bytes 2973696 | tf_op jit(solution)/shard_map/all_to_all | solution.py:163
  (127 shorter events, 47.8 us)
Async XLA Ops:
  0.0 6.5 %copy-start.16 = (f32[11,11,1,1,1]{1,0,4,3,2:T(8,128)S(1)}, f32[11,11,1,1,1]{1,0,4,3,2:T(8,128)}, u32[]{:S(2)}) copy-start(f32[11,11,1,1,1]{1,0,4,3,2:T(8,128)} %constant.689) | copy-start | bytes 1456
  0.0 3.8 copy-start.3
  32.5 34.4 %copy-start.4 = (f32[11,11]{1,0:T(8,128)S(1)}, f32[11,11]{1,0:T(8,128)}, u32[]{:S(2)}) copy-start(f32[11,11]{1,0:T(8,128)} %constant.672.clone) | copy-start | bytes 1456
  32.5 35.2 %copy-start.14 = (f32[11]{0:T(128)S(1)}, f32[11]{0:T(128)}, u32[]{:S(2)}) copy-start(f32[11]{0:T(128)} %constant.671.clone) | copy-start | bytes 136
  32.5 35.3 %copy-start.15 = (f32[11,11,1,32]{3,2,1,0:T(1,128)S(1)}, f32[11,11,1,32]{3,2,1,0:T(1,128)}, u32[]{:S(2)}) copy-start(f32[11,11,1,32]{3,2,1,0:T(1,128)} %param.62) | copy-start | bytes 46468
  59.5 37.8 %all-to-all-start = ((f32[16,1,23232]{2,1,0:T(1,128)}), f32[16,1,23232]{2,1,0:T(1,128)S(1)}, u32[]{:S(2)}, u32[]{:S(2)}) async-start(f32[16,1,23232]{2,1,0:T(1,128)} %reshape.1407), calls=%async_computation | async-start | bytes 2981888 | tf_op jit(solution)/shard_map/all_to_all | solution.py:150
  73.4 0.7 copy-start.11
  74.2 3.6 copy-start.12
  75.7 1.3 copy-start.6
  200.1 23.3 %all-to-all-start.1 = ((f32[2,1,185856]{2,1,0:T(1,128)}), f32[2,1,185856]{2,1,0:T(1,128)S(1)}, u32[]{:S(2)}, u32[]{:S(2)}) async-start(f32[2,1,185856]{2,1,0:T(1,128)} %reshape.1409), calls=%async_computation.1 | async-start | bytes 2973696 | tf_op jit(solution)/shard_map/all_to_all | solution.py:149
  251.0 1.6 copy-start.5
  252.6 1.1 copy-start.13
  292.8 5.5 copy-start.10
  363.1 14.2 %copy-start = (f32[16,3,11,11,2,32]{5,0,3,4,2,1:T(8,128)S(1)}, f32[16,3,11,11,2,32]{5,0,3,4,2,1:T(8,128)}, u32[]{:S(2)}) copy-start(f32[16,3,11,11,2,32]{5,0,3,4,2,1:T(8,128)} %copy_add_fusion.1) | copy-start | bytes 4460548
  401.9 4.3 slice-start.2
  402.0 4.2 copy-start.9
  402.6 4.9 slice-start.3
  403.1 3.0 copy-start.2
  413.1 29.0 %copy-start.1 = (f32[16,3,11,11,2,32]{5,0,3,4,2,1:T(8,128)}, f32[16,3,11,11,2,32]{5,0,3,4,2,1:T(8,128)S(1)}, u32[]{:S(2)}) copy-start(f32[16,3,11,11,2,32]{5,0,3,4,2,1:T(8,128)S(1)} %multiply_add_fusion.1) | copy-start | bytes 4460548
  455.8 5.7 copy-start.8
  476.9 14.2 %slice-start = ((s8[5947392]{0:T(1024)(128)(4,1)}), s8[4194304]{0:T(1024)(128)(4,1)S(1)}, s32[]{:S(2)}) async-start(s8[5947392]{0:T(1024)(128)(4,1)} %bitcast.331), calls=%async_computation.3 | async-start | bytes 8388608
  476.9 14.2 %slice-start.1 = ((s8[5947392]{0:T(1024)(128)(4,1)}), s8[1753088]{0:T(1024)(128)(4,1)S(1)}, s32[]{:S(2)}) async-start(s8[5947392]{0:T(1024)(128)(4,1)} %bitcast.331), calls=%async_computation.4 | async-start | bytes 3506176
  518.8 5.7 copy-start.7
where the time goes:
time: 597 us; the launch traced here: 585 us
  local copies, waits for them, and re-layouts  200 us (34%)
  other arithmetic  167 us (28%)
  matrix products  152 us (25%)
  waiting for transfers between devices  27.7 us (5%)
  blocking collectives  26.9 us (5%)
  starting transfers between devices  11 us (2%)
    unnamed x50, local copies, waits for them, and re-layouts  115 us
    dot_general x5, matrix products, helm_apply(): jnp.einsum('ia,rcabxy->rcibxy', stiff_mat, field, precision=lax.Precision...  71.9 us
    dot_general x5, matrix products, helm_apply(): jnp.einsum('jb,rcabxy->rcajxy', stiff_mat, field, precision=lax.Precision...  70.4 us
    add x5, other arithmetic, helm_apply(): return along_first + along_second + coeff * field  57.5 us
    all_to_all x3, local copies, waits for them, and re-layouts, per_device(): lax.all_to_all(spectra, 'mode', split_axis=0, concat_axis=5, tiled=True)  33.7 us
    add x3, other arithmetic, chebyshev(): recurrence_next * recurrence * direction  31.8 us
    all_to_all x1, blocking collectives, per_device(): lax.all_to_all(solved, 'mesh', split_axis=4, concat_axis=0, tiled=True)  21.3 us
    dot_general x1, local copies, waits for them, and re-layouts, per_device(): jnp.einsum('cabxyz,zk->kcabxy', forcing, table, precision=lax.Precision.H...  18.8 us
  transfers between devices with their start and end apart: 2, of which 2 were waited for; matrix products, arithmetic and copies ran while one was open for 3% of the time, Pallas kernels for 0%

commit v1 on v0

v1 whole, which is shorter than its diff:
```python
import functools
import math

import jax
import jax.numpy as jnp
import numpy as np
from jax import lax
from jax.experimental import pallas as pl
from jax.experimental.pallas import tpu as pltpu
from jax.sharding import PartitionSpec as P

MODES = 256
ITERS = 6
LANES = 128
CHUNKS = ((0, 1), (2,))

helm_base = 1.0
span_wave = 0.02
bound_ratio = 25.0


def legendre_pair(points, order):
    previous = points * 0.0 + 1.0
    current = points * 1.0
    for degree in range(2, order + 1):
        following = ((2 * degree - 1) * points * current - (degree - 1) * previous) / degree
        previous = current
        current = following
    return (current, previous)


def gll_tables(order):
    count = order + 1
    points = -np.cos(np.pi * np.arange(count) / order)
    for sweep in range(200):
        top_vals, below_vals = legendre_pair(points, order)
        points = points - (points * top_vals - below_vals) / (count * top_vals)
    legendre_vals, below_vals = legendre_pair(points, order)
    weights = 2.0 / (order * (order + 1) * legendre_vals**2)
    identity = np.eye(count)
    spacing = points[:, None] - points[None, :] + identity
    derivative = legendre_vals[:, None] / (legendre_vals[None, :] * spacing) * (1.0 - identity)
    corner = np.concatenate(
        [[-order * (order + 1) / 4.0], np.zeros(order - 1), [order * (order + 1) / 4.0]]
    )
    derivative = derivative + identity * corner[None, :]
    stiffness = derivative.T @ (weights[:, None] * derivative)
    weight_mat = identity * weights[None, :]
    laplace = np.kron(stiffness, weight_mat) + np.kron(weight_mat, stiffness)
    lap_diag = np.diagonal(laplace)
    upper_bound = float(np.max(np.sum(np.abs(laplace), axis=1) / lap_diag))
    return (weights, derivative, laplace, lap_diag, upper_bound)


def split_table(table):
    table = np.asarray(table, np.float64)
    high = table.astype(jnp.bfloat16)
    low = (table - high.astype(np.float64)).astype(jnp.bfloat16)
    return (high, low)


def split_value(value):
    high = value.astype(jnp.bfloat16)
    low = (value - high.astype(jnp.float32)).astype(jnp.bfloat16)
    return (high, low)


def dft_table(planes):
    turns = np.arange(planes)[None, :] * np.arange(MODES)[:, None] % planes
    angles = 2.0 * np.pi / planes * turns
    return np.concatenate([np.cos(angles), -np.sin(angles)], axis=0) / math.sqrt(planes)


def padded(table, shape):
    result = np.zeros(shape, np.float64)
    result[tuple(slice(0, n) for n in table.shape)] = table
    return result


def dot(a, b, contract=((1,), (0,))):
    return lax.dot_general(a, b, (contract, ((), ())), preferred_element_type=jnp.float32)


def front_kernel(first, second, field, grad_hi, grad_cat, mass, dft_hi, dft_lo, out):
    local, rows, planes = field.shape[1:]
    forcing = []
    for e in range(local):
        value = field[0, e]
        high, low = split_value(value)
        grad = dot(grad_cat[...], jnp.concatenate([high, high], axis=0)) + dot(grad_hi[...], low)
        forcing.append((value - (first[0, e] * grad[:rows] + second[0, e] * grad[rows:])) * mass[...])
    both = ((1,), (1,))
    kept = out.shape[3]
    for start in range(0, local, 2):
        pair = forcing[start : start + 2]
        high, low = split_value(jnp.concatenate(pair, axis=0))
        spectra = (
            dot(dft_hi[...], high, both)
            + dot(dft_hi[...], low, both)
            + dot(dft_lo[...], high, both)
        )
        for i in range(len(pair)):
            part = spectra[:, i * rows : (i + 1) * rows]
            out[:, 0, start + i] = part.reshape(out.shape[0], kept, rows)


def front(planes_first, first, count, tables, peers):
    comps, local, rows, planes = planes_first.shape
    kept = tables[-1].shape[0] // peers

    def pick(index):
        return pl.BlockSpec((1, local, rows, planes), lambda c: (index(c), 0, 0, 0))

    def whole(table):
        return pl.BlockSpec(table.shape, lambda c: (0,) * table.ndim)

    return pl.pallas_call(
        front_kernel,
        out_shape=jax.ShapeDtypeStruct((peers, count, local, kept, rows), jnp.float32),
        grid=(count,),
        in_specs=[pick(lambda c: 0), pick(lambda c: 1), pick(lambda c: c + first)]
        + [whole(t) for t in tables],
        out_specs=pl.BlockSpec((peers, 1, local, kept, rows), lambda c: (0, c, 0, 0, 0)),
        name=f"front{first}",
    )(planes_first, planes_first, planes_first, *tables)


def shared_sums(tiles, masks):
    top, bottom, right, left = masks
    summed = []
    for column in tiles:
        line = []
        for row, value in enumerate(column):
            after = column[row + 1] if row + 1 < len(column) else None
            before = column[row - 1] if row > 0 else None
            extra = 0.0
            if before is not None:
                extra = jnp.where(bottom, pltpu.roll(before, LANES - 10, 1), extra)
            if after is not None:
                extra = jnp.where(top, pltpu.roll(after, 10, 1), extra)
            line.append(value + extra)
        summed.append(line)
    result = []
    for col, line in enumerate(summed):
        values = []
        for row, value in enumerate(line):
            extra = 0.0
            if col > 0:
                extra = jnp.where(left, pltpu.roll(summed[col - 1][row], LANES - 110, 1), extra)
            if col + 1 < len(summed):
                extra = jnp.where(right, pltpu.roll(summed[col + 1][row], 110, 1), extra)
            values.append(value if isinstance(extra, float) else value + extra)
        result.append(values)
    return result


def read_masks(mask_ref):
    return tuple(mask_ref[i] > 0.5 for i in range(4))


def places(shape, kept):
    groups, owners, local_cols, local_rows = shape
    table = []
    for col in range(owners * local_cols):
        owner, lc = divmod(col, local_cols)
        line = []
        for row in range(groups * local_rows):
            part, e = divmod(row, local_rows)
            line.append((((part * owners + owner) * local_cols + lc) * local_rows + e) * kept)
        table.append(line)
    return table


def prep_kernel(shape, wave_ref, pen_ref, lap_ref, mask_ref, inverse_ref):
    masks = read_masks(mask_ref)
    kept = wave_ref.shape[0]
    where = places(shape, kept)
    base = wave_ref[...] + lap_ref[...]
    tiles = [
        [base + pen_ref[col, row : row + 1, :] for row in range(len(where[col]))]
        for col in range(len(where))
    ]
    for line, rows in zip(shared_sums(tiles, masks), where):
        for value, first in zip(line, rows):
            inverse_ref[first : first + kept, :] = 1.0 / value


def solve_kernel(
    shape, midpoint, spot_ref, gain_ref, src_ref, inverse_ref, mat_ref, mask_ref, *rest
):
    groups, owners, local_cols, local_rows = shape
    outs = rest[:-4]
    work_ref, res_ref, dir_ref, sum_ref = rest[-4:]
    masks = read_masks(mask_ref)
    kept = src_ref.shape[-2]
    where = places(shape, kept)
    cols, rows_all = len(where), len(where[0])
    total = cols * rows_all * kept
    block = total // math.gcd(groups, 4)

    def tile(ref, col, row):
        return ref[pl.ds(where[col][row], kept), :]

    def pieces(ref):
        return [[tile(ref, col, row) for row in range(rows_all)] for col in range(cols)]

    def source(col, row):
        owner, lc = divmod(col, local_cols)
        part, e = divmod(row, local_rows)
        return src_ref[part, owner, 0, lc * local_rows + e]

    first = shared_sums(
        [[source(col, row) for row in range(rows_all)] for col in range(cols)], masks
    )
    for col in range(cols):
        for row in range(rows_all):
            here = pl.ds(where[col][row], kept)
            residual = inverse_ref[here, :] * first[col][row]
            direction = residual * (1.0 / midpoint)
            res_ref[here, :] = residual
            dir_ref[here, :] = direction
            sum_ref[pl.ds((col * rows_all + row) * kept, kept), :] = direction

    def sweep(step, carry):
        keep = gain_ref[step, 0]
        gain = gain_ref[step, 1]
        for start in range(0, total, block):
            high, low = split_value(dir_ref[pl.ds(start, block), :])
            product = dot(jnp.concatenate([high, low], axis=1), mat_ref[...])
            work_ref[pl.ds(start, block), :] = product[:, :LANES] + product[:, LANES:]
        summed = shared_sums(pieces(work_ref), masks)
        for col in range(cols):
            for row in range(rows_all):
                here = pl.ds(where[col][row], kept)
                direction = dir_ref[here, :]
                residual = res_ref[here, :] - direction - inverse_ref[here, :] * summed[col][row]
                direction = keep * direction + gain * residual
                res_ref[here, :] = residual
                dir_ref[here, :] = direction
                there = pl.ds((col * rows_all + row) * kept, kept)
                sum_ref[there, :] = sum_ref[there, :] + direction
        return carry

    lax.fori_loop(0, ITERS - 1, sweep, 0)

    spot = spot_ref[0]
    for shift, out in enumerate(outs):
        for lc in range(local_cols):
            col = lax.rem(spot + shift, owners) * local_cols + lc
            for k in range(kept):
                out[k, lc] = sum_ref[pl.ds(col * (rows_all * kept) + k, rows_all, stride=kept), :]


def solve(shape, midpoint, component, slot, spot, gains, moved, inverse, mat, masks):
    groups, owners, local_cols, local_rows = shape
    kept = moved.shape[-2]
    rows = groups * local_rows
    total = owners * local_cols * rows * kept
    piece = jax.ShapeDtypeStruct((kept, local_cols, rows, LANES), jnp.float32)
    smem = pl.BlockSpec(memory_space=pltpu.SMEM)
    vmem = pl.BlockSpec(memory_space=pltpu.VMEM)
    block = moved.shape[:2] + (1,) + moved.shape[3:]
    return pl.pallas_call(
        functools.partial(solve_kernel, shape, midpoint),
        out_shape=[piece] * owners,
        grid=(1,),
        in_specs=[
            smem,
            smem,
            pl.BlockSpec(block, lambda i: (0, 0, slot, 0, 0, 0)),
            vmem,
            vmem,
            vmem,
        ],
        out_specs=[vmem] * owners,
        scratch_shapes=[pltpu.VMEM((total, LANES), jnp.float32)] * 4,
        name=f"solve{component}",
    )(spot, gains, moved, inverse, mat, masks)


def finish_kernel(component, place_ref, src_ref, *rest):
    out_ref, stage_ref, sems = rest[-3:]
    nodes = stage_ref.shape[1]
    kept = src_ref.shape[0]
    copies = []
    for k in range(kept):
        for lc in range(src_ref.shape[1]):
            stage_ref[k, :, lc, :] = src_ref[k, lc].T[:nodes]
        target = out_ref.at[place_ref[0] * kept + k, component]
        copy = pltpu.make_async_copy(stage_ref.at[k], target, sems.at[k])
        copy.start()
        copies.append(copy)
    for copy in copies:
        copy.wait()


def finish(place, component, comps, modes, nodes, source, so_far):
    kept, local_cols, rows, lanes = source.shape
    keep_out = pl.BlockSpec(memory_space=pl.ANY)
    in_specs = [pl.BlockSpec(memory_space=pltpu.SMEM), pl.BlockSpec(memory_space=pltpu.VMEM)]
    args = [place, source]
    aliases = {}
    if so_far is not None:
        in_specs.append(keep_out)
        args.append(so_far)
        aliases = {2: 0}
    return pl.pallas_call(
        functools.partial(finish_kernel, component),
        out_shape=jax.ShapeDtypeStruct((modes, comps, nodes, local_cols, rows), jnp.float32),
        in_specs=in_specs,
        out_specs=keep_out,
        scratch_shapes=[
            pltpu.VMEM((kept, nodes, local_cols, rows), jnp.float32),
            pltpu.SemaphoreType.DMA((kept,)),
        ],
        input_output_aliases=aliases,
        name=f"finish{component}",
    )(*args)


def per_device(velocity, penalty):
    comps, count, _, local_cols, local_rows, planes = velocity.shape
    nodes = count * count
    groups = lax.axis_size("mode")
    owners = lax.axis_size("mesh")
    peers = groups * owners
    spot = lax.axis_index("mesh")
    local = local_cols * local_rows
    kept = 2 * MODES // peers
    total_cols = owners * local_cols
    total_rows = groups * local_rows

    weights, derivative, laplace, lap_diag, upper_bound = gll_tables(count - 1)
    mass = np.kron(weights, weights)
    lower_bound = upper_bound / bound_ratio
    midpoint = (upper_bound + lower_bound) / 2.0
    half_width = (upper_bound - lower_bound) / 2.0
    recurrence = half_width / midpoint
    gains = []
    for step in range(1, ITERS):
        following = 1.0 / (2.0 * midpoint / half_width - recurrence)
        gains.append((following * recurrence, 2.0 * following / half_width))
        recurrence = following
    gains = jnp.asarray(np.array(gains), jnp.float32)
    identity = np.eye(count)
    grads = np.concatenate(
        [
            padded(np.kron(derivative, identity), (LANES, LANES)),
            padded(np.kron(identity, derivative), (LANES, LANES)),
        ]
    )
    grad_hi, grad_lo = split_table(grads)
    dft_hi, dft_lo = split_table(dft_table(planes))
    mass_col = padded(mass[:, None], (LANES, 1)).astype(np.float32)
    grad_cat = np.concatenate([grad_hi, grad_lo], axis=1)
    front_tables = [jnp.asarray(t) for t in (grad_hi, grad_cat, mass_col, dft_hi, dft_lo)]
    off_diag = laplace.T - np.diag(lap_diag)
    mat_hi, mat_lo = split_table(padded(off_diag, (LANES, LANES)))
    half = np.concatenate([mat_hi, mat_lo], axis=1)
    mat = jnp.asarray(np.concatenate([half, half], axis=0))
    node = np.arange(LANES)
    real = node < nodes
    masks = np.stack(
        [
            real & (node % count == count - 1),
            real & (node % count == 0),
            real & (node // count == count - 1),
            real & (node // count == 0),
        ]
    ).astype(np.float32)
    masks = jnp.asarray(np.broadcast_to(masks[:, None], (4, kept, LANES)))
    lap_row = np.ones((1, LANES))
    lap_row[0, :nodes] = lap_diag
    lap_row = jnp.asarray(lap_row, jnp.float32)
    mass_row = jnp.asarray(padded(mass[None], (1, LANES)), jnp.float32)

    own = penalty.reshape(nodes, local_cols, total_rows).transpose(1, 2, 0)
    own = jnp.pad(own, ((0, 0), (0, 0), (0, LANES - nodes))) * mass_row
    full = jnp.zeros((total_cols, total_rows, LANES), jnp.float32)
    full = lax.dynamic_update_slice(full, own, (spot * local_cols, 0, 0))
    for shift in range(1, owners):
        ring = [(i, (i + shift) % owners) for i in range(owners)]
        other = lax.ppermute(own, "mesh", ring)
        full = lax.dynamic_update_slice(
            full, other, (lax.rem(spot + owners - shift, owners) * local_cols, 0, 0)
        )
    first_row = (lax.axis_index("mode") * owners + spot) * kept
    wave = ((first_row + jnp.arange(kept, dtype=jnp.int32)) % MODES).astype(jnp.float32)
    helm = helm_base + (span_wave * wave) ** 2
    wave_mass = helm[:, None] * mass_row

    shape = (groups, owners, local_cols, local_rows)
    total = peers * local * kept
    inverse = pl.pallas_call(
        functools.partial(prep_kernel, shape),
        out_shape=jax.ShapeDtypeStruct((total, LANES), jnp.float32),
        name="prep",
    )(wave_mass, full, lap_row, masks)

    planes_first = velocity.reshape(comps, nodes, local, planes).transpose(0, 2, 1, 3)
    planes_first = jnp.pad(planes_first, ((0, 0), (0, 0), (0, LANES - nodes), (0, 0)))

    spot_arg = spot.astype(jnp.int32)[None]
    result = None
    for chunk in CHUNKS:
        spectra = front(planes_first, chunk[0], len(chunk), front_tables, peers)
        moved = lax.all_to_all(spectra, ("mode", "mesh"), split_axis=0, concat_axis=0, tiled=True)
        moved = moved.reshape((groups, owners) + moved.shape[1:])
        for slot, component in enumerate(chunk):
            solved = solve(
                shape, midpoint, component, slot, spot_arg, gains, moved, inverse, mat, masks
            )
            for shift in range(owners):
                part = solved[shift]
                if shift:
                    ring = [(i, (i + shift) % owners) for i in range(owners)]
                    part = lax.ppermute(part, "mesh", ring)
                place = lax.rem(spot_arg + (owners - shift), owners)
                result = finish(place, component, comps, kept * owners, nodes, part, result)
    return result.reshape(kept * owners, comps, count, count, local_cols, total_rows)


def solution(mesh):
    return jax.shard_map(
        per_device,
        mesh=mesh,
        in_specs=(P(None, None, None, "mesh", "mode", None), P(None, None, "mesh", None)),
        out_specs=P("mode", None, None, None, "mesh", None),
        check_vma=False,
    )
```

time: 597 us -> 92.4 us (0.15); the launches traced: 585 us -> 91.7 us
  local copies, waits for them, and re-layouts: 200 us -> 6.52 us
  other arithmetic: 167 us -> 0.69 us
  matrix products: 152 us -> 0 us
  Pallas kernels: 0 us -> 43.4 us
  blocking collectives: 26.9 us -> 0 us
    dot_general x13 -> x0, matrix products: 152 us -> none  [the longest x5 71.9 us: helm_apply(): jnp.einsum('ia,rcabxy->rcibxy', stiff_mat, field, precision=lax.Precision...]
    unnamed x50 -> x18, local copies, waits for them, and re-layouts: 115 us -> 2.9 us
    add x19 -> x1, other arithmetic: 99 us -> 0.01 us  [per_device(): helm = helm_base + (span_wave * wave) ** 2]
    all_to_all x6 -> x0, local copies, waits for them, and re-layouts: 48.1 us -> none  [the longest x3 33.7 us: per_device(): lax.all_to_all(spectra, 'mode', split_axis=0, concat_axis=5, tiled=True)]
    pallas_call x0 -> x12, Pallas kernels: none -> 43.4 us  [the longest x3 18.4 us: solve(): pl.pallas_call(functools.partial(solve_kernel, shape, midpoint), out_shap...]
    all_to_all x4 -> x0, other arithmetic: 23.9 us -> none  [the longest x2 12.7 us: per_device(): lax.all_to_all(spectra, 'mode', split_axis=0, concat_axis=5, tiled=True)]
    all_to_all x1 -> x0, blocking collectives: 21.3 us -> none  [per_device(): lax.all_to_all(solved, 'mesh', split_axis=4, concat_axis=0, tiled=True)]
    dot_general x1 -> x0, local copies, waits for them, and re-layouts: 18.8 us -> none  [per_device(): jnp.einsum('cabxyz,zk->kcabxy', forcing, table, precision=lax.Precision.H...]
  transfers between devices with their start and end apart: 2 -> 6, of which waited for: 2 -> 2; matrix products, arithmetic and copies ran while one was open for 3% -> 2% of each run, Pallas kernels for 0% -> 40%
where the time goes in v1:
time: 92.4 us; the launch traced here: 91.7 us
  Pallas kernels  43.4 us (47%)
  waiting for transfers between devices  24.3 us (26%)
  starting transfers between devices  16.6 us (18%)
  local copies, waits for them, and re-layouts  6.52 us (7%)
    all_to_all x2, waiting for transfers between devices, per_device(): lax.all_to_all(spectra, ('mode', 'mesh'), split_axis=0, concat_axis=0, ti...  22.6 us
    pallas_call x3, Pallas kernels, solve(): pl.pallas_call(functools.partial(solve_kernel, shape, midpoint), out_shap...  18.4 us
    pallas_call x6, Pallas kernels, finish(): pl.pallas_call(functools.partial(finish_kernel, component), out_shape=jax...  14.6 us
    all_to_all x2, starting transfers between devices, per_device(): lax.all_to_all(spectra, ('mode', 'mesh'), split_axis=0, concat_axis=0, ti...  11 us
    pallas_call x2, Pallas kernels, front(): pl.pallas_call(front_kernel, out_shape=jax.ShapeDtypeStruct((peers, count...  8.36 us
    ppermute x3, starting transfers between devices, per_device(): part = lax.ppermute(part, 'mesh', ring)  3.81 us
    unnamed x18, local copies, waits for them, and re-layouts  2.9 us
    pallas_call x1, Pallas kernels, per_device(): pl.pallas_call(functools.partial(prep_kernel, shape), out_shape=jax.Shape...  2.08 us
  transfers between devices with their start and end apart: 6, of which 2 were waited for; matrix products, arithmetic and copies ran while one was open for 2% of the time, Pallas kernels for 40%

profile of v1, /device:TPU:0, one launch (start us, length us, event | category | flops | bytes accessed | tf_op | source)
XLA Modules:
  0.0 91.7 jit_solution(11572255197317455114)
XLA Ops:
  0.0 1.7 %copy.23 = f32[3,121,2,512]{3,1,2,0:T(8,128)S(1)} copy(f32[3,121,2,512]{3,2,1,0:T(2,128)} %bitcast.14) | data formatting | bytes 2973696 | tf_op jit(solution)/shard_map/reshape | solution.py:400
  1.7 1.3 %pad.8.first.second.field = f32[3,2,128,512]{3,2,1,0:T(8,128)} pad(f32[3,2,121,512]{3,2,1,0:T(8,128)S(1)} %bitcast.12, f32[]{:T(128)} %constant.63.clone.1), padding=0_0x0_0x0_7x0_0 | pad | bytes 3059716 | tf_op jit(solution)/shard_map/jit(_pad)/pad | solution.py:401
  2.9 4.8 %front0.1 = f32[32,2,2,16,128]{4,3,2,1,0:T(8,128)} custom-call(f32[3,2,128,512]{3,2,1,0:T(8,128)} %pad.8.first.second.field, f32[3,2,128,512]{3,2,1,0:T(8,128)} %pad.8.first.second.field, f32[3,2,128,512]{3,2,1,0:T(8,128)} %pad.8.first.second.field, bf16[256,128]{1,0:T(8,128)(2,1)} %constant.75.clone.grad_hi, bf16[256,256]{1,0:T(8,128)(2,1)} %constant.76.clone.grad_cat, ...), custom_call_target="tpu_custom_call" | custom-call | tf_op jit(solution)/shard_map/front0/pallas_call | solution.py:117
  7.7 0.0 copy-start.6
  7.7 0.0 copy-start.7
  7.7 0.0 copy-start.8
  7.7 7.3 %all-to-all-start.1 = ((f32[32,2,2,16,128]{4,3,2,1,0:T(8,128)}), f32[32,2,2,16,128]{4,3,2,1,0:T(8,128)S(1)}, u32[]{:S(2)}, u32[]{:S(2)}) async-start(f32[32,2,2,16,128]{4,3,2,1,0:T(8,128)} %front0.1), calls=%async_computation.1 | async-start | bytes 2097152 | tf_op jit(solution)/shard_map/all_to_all | solution.py:407
  15.1 3.6 %front2.1 = f32[32,1,2,16,128]{4,3,2,1,0:T(8,128)} custom-call(f32[3,2,128,512]{3,2,1,0:T(8,128)} %pad.8.first.second.field, f32[3,2,128,512]{3,2,1,0:T(8,128)} %pad.8.first.second.field, f32[3,2,128,512]{3,2,1,0:T(8,128)} %pad.8.first.second.field, bf16[256,128]{1,0:T(8,128)(2,1)} %constant.75.clone.grad_hi, bf16[256,256]{1,0:T(8,128)(2,1)} %constant.76.clone.grad_cat, ...), custom_call_target="tpu_custom_call" | custom-call | tf_op jit(solution)/shard_map/front2/pallas_call | solution.py:117
  18.7 22.6 %all-to-all-done.1 = f32[32,2,2,16,128]{4,3,2,1,0:T(8,128)S(1)} async-done(((f32[32,2,2,16,128]{4,3,2,1,0:T(8,128)}), f32[32,2,2,16,128]{4,3,2,1,0:T(8,128)S(1)}, u32[]{:S(2)}, u32[]{:S(2)}) %all-to-all-start.1) | async-done | bytes 1048608 | tf_op jit(solution)/shard_map/all_to_all | solution.py:407
  41.3 0.0 copy-start
  41.3 3.6 %all-to-all-start = ((f32[32,1,2,16,128]{4,3,2,1,0:T(8,128)}), f32[32,1,2,16,128]{4,3,2,1,0:T(8,128)S(1)}, u32[]{:S(2)}, u32[]{:S(2)}) async-start(f32[32,1,2,16,128]{4,3,2,1,0:T(8,128)} %front2.1), calls=%async_computation | async-start | bytes 1048576 | tf_op jit(solution)/shard_map/all_to_all | solution.py:407
  44.9 0.0 copy-done.6
  44.9 0.1 copy.21
  45.0 0.0 copy-done.7
  45.0 1.8 %collective-permute-start = (f32[1,32,128]{2,1,0:T(8,128)S(1)}, f32[1,32,128]{2,1,0:T(8,128)S(1)}, u32[]{:S(2)}, u32[]{:S(2)}) collective-permute-start(f32[1,32,128]{2,1,0:T(8,128)S(1)} %get-tuple-element.17), channel_id=1, source_target_pairs={{0,1},{1,0},{2,3},{3,2},{4,5},{5,4},{6,7},{7,6},{8,9},{9,8},{10,11... | collective-permute-start | bytes 49160 | tf_op jit(solution)/shard_map/ppermute | solution.py:383
  46.9 0.7 broadcast_multiply_fusion.wave_ref
  47.5 1.6 %collective-permute-done = f32[1,32,128]{2,1,0:T(8,128)S(1)} collective-permute-done((f32[1,32,128]{2,1,0:T(8,128)S(1)}, f32[1,32,128]{2,1,0:T(8,128)S(1)}, u32[]{:S(2)}, u32[]{:S(2)}) %collective-permute-start) | collective-permute-done | bytes 16416 | tf_op jit(solution)/shard_map/ppermute | solution.py:383
  49.2 0.0 copy-done.8
  49.2 0.0 copy-start.5
  49.2 0.6 jit_solution_.3.mask_ref
  49.8 0.0 copy-done.5
  49.8 2.1 %prep.1.inverse_ref = f32[1024,128]{1,0:T(8,128)} custom-call(f32[16,128]{1,0:T(8,128)} %broadcast_multiply_fusion.wave_ref, f32[2,32,128]{2,1,0:T(8,128)} %copy-done.5, f32[1,128]{1,0:T(1,128)} %constant.82.clone.lap_ref, f32[4,16,128]{2,1,0:T(8,128)} %jit_solution_.3.mask_ref), custom_call_target="tpu_custom_call" | custom-call | tf_op jit(solution)/shard_map/prep/pallas_call | solution.py:394
  51.9 0.0 copy-done
  51.9 6.1 %solve0.1 = (f32[16,1,32,128]{3,2,1,0:T(8,128)}, f32[16,1,32,128]{3,2,1,0:T(8,128)}) custom-call(s32[1]{0:T(128)} %bitcast.spot_ref, f32[5,2]{1,0:T(8,128)} %constant.74.clone.gain_ref, f32[16,2,2,2,16,128]{5,4,3,2,1,0:T(8,128)} %bitcast.10, f32[1024,128]{1,0:T(8,128)} %prep.1.inverse_ref, bf16[256,256]{1,0:T(8,128)(2,1)} %constant.80.clone.mat_ref, ...), custom_call_target="tpu_custom_call" | custom-call | tf_op jit(solution)/shard_map/solve0/pallas_call | solution.py:263
  58.0 1.8 %collective-permute-start.3 = (f32[16,1,32,128]{3,2,1,0:T(8,128)}, f32[16,1,32,128]{3,2,1,0:T(8,128)S(1)}, u32[]{:S(2)}, u32[]{:S(2)}) collective-permute-start(f32[16,1,32,128]{3,2,1,0:T(8,128)} %get-tuple-element.15), channel_id=1, source_target_pairs={{0,1},{1,0},{2,3},{3,2},{4,5},{5,4},{6,7},{7,6},{8,9},{9,8},{10,11... | collective-permute-start | bytes 786440 | tf_op jit(solution)/shard_map/ppermute | solution.py:417
  59.8 6.1 %solve1.1 = (f32[16,1,32,128]{3,2,1,0:T(8,128)}, f32[16,1,32,128]{3,2,1,0:T(8,128)}) custom-call(s32[1]{0:T(128)} %bitcast.spot_ref, f32[5,2]{1,0:T(8,128)} %constant.74.clone.gain_ref, f32[16,2,2,2,16,128]{5,4,3,2,1,0:T(8,128)} %bitcast.11, f32[1024,128]{1,0:T(8,128)} %prep.1.inverse_ref, bf16[256,256]{1,0:T(8,128)(2,1)} %constant.80.clone.mat_ref, ...), custom_call_target="tpu_custom_call" | custom-call | tf_op jit(solution)/shard_map/solve1/pallas_call | solution.py:263
  65.9 0.2 collective-permute-start.2
  66.2 0.0 all-to-all-done
  66.2 0.0 copy-start.1
  66.2 0.8 copy-done.1
  67.0 6.1 %solve2.1 = (f32[16,1,32,128]{3,2,1,0:T(8,128)}, f32[16,1,32,128]{3,2,1,0:T(8,128)}) custom-call(s32[1]{0:T(128)} %bitcast.spot_ref, f32[5,2]{1,0:T(8,128)} %constant.74.clone.gain_ref, f32[16,2,1,2,16,128]{5,4,3,2,1,0:T(8,128)} %bitcast.13, f32[1024,128]{1,0:T(8,128)} %prep.1.inverse_ref, bf16[256,256]{1,0:T(8,128)(2,1)} %constant.80.clone.mat_ref, ...), custom_call_target="tpu_custom_call" | custom-call | tf_op jit(solution)/shard_map/solve2/pallas_call | solution.py:263
  73.1 1.8 %collective-permute-start.1 = (f32[16,1,32,128]{3,2,1,0:T(8,128)}, f32[16,1,32,128]{3,2,1,0:T(8,128)S(1)}, u32[]{:S(2)}, u32[]{:S(2)}) collective-permute-start(f32[16,1,32,128]{3,2,1,0:T(8,128)} %get-tuple-element.11), channel_id=1, source_target_pairs={{0,1},{1,0},{2,3},{3,2},{4,5},{5,4},{6,7},{7,6},{8,9},{9,8},{10,11... | collective-permute-start | bytes 786440 | tf_op jit(solution)/shard_map/ppermute | solution.py:417
  74.9 2.4 %finish0.2.rest_0_ = f32[32,3,121,1,32]{4,3,2,1,0:T(1,128)} custom-call(s32[1]{0:T(128)S(6)} %rem.89.place_ref, f32[16,1,32,128]{3,2,1,0:T(8,128)} %get-tuple-element.16.src_ref), custom_call_target="tpu_custom_call" | custom-call | tf_op jit(solution)/shard_map/finish0/pallas_call | solution.py:307
  77.3 0.0 collective-permute-done.3.src_ref
  77.3 0.0 copy-start.3
  77.3 0.7 copy-done.3
  78.0 2.4 %finish0.3.rest_0_ = f32[32,3,121,1,32]{4,3,2,1,0:T(1,128)} custom-call(s32[1]{0:T(128)S(6)} %rem.69.place_ref, f32[16,1,32,128]{3,2,1,0:T(8,128)} %copy-done.3, f32[32,3,121,1,32]{4,3,2,1,0:T(1,128)} %finish0.2.rest_0_), custom_call_target="tpu_custom_call", output_to_operand_aliasing={{}: (2, {})} | custom-call | tf_op jit(solution)/shard_map/finish0/pallas_call | solution.py:307
  80.5 2.4 %finish1.2.rest_0_ = f32[32,3,121,1,32]{4,3,2,1,0:T(1,128)} custom-call(s32[1]{0:T(128)S(6)} %rem.89.place_ref, f32[16,1,32,128]{3,2,1,0:T(8,128)} %get-tuple-element.14.src_ref, f32[32,3,121,1,32]{4,3,2,1,0:T(1,128)} %finish0.3.rest_0_), custom_call_target="tpu_custom_call", output_to_operand_aliasing={{}: (2, {})} | custom-call | tf_op jit(solution)/shard_map/finish1/pallas_call | solution.py:307
  82.9 0.0 collective-permute-done.2.src_ref
  82.9 0.0 copy-start.2
  82.9 0.7 copy-done.2
  83.6 2.4 %finish1.3.rest_0_ = f32[32,3,121,1,32]{4,3,2,1,0:T(1,128)} custom-call(s32[1]{0:T(128)S(6)} %rem.69.place_ref, f32[16,1,32,128]{3,2,1,0:T(8,128)} %copy-done.2, f32[32,3,121,1,32]{4,3,2,1,0:T(1,128)} %finish1.2.rest_0_), custom_call_target="tpu_custom_call", output_to_operand_aliasing={{}: (2, {})} | custom-call | tf_op jit(solution)/shard_map/finish1/pallas_call | solution.py:307
  86.1 2.4 %finish2.2.rest_0_ = f32[32,3,121,1,32]{4,3,2,1,0:T(1,128)} custom-call(s32[1]{0:T(128)S(6)} %rem.89.place_ref, f32[16,1,32,128]{3,2,1,0:T(8,128)} %get-tuple-element.12.src_ref, f32[32,3,121,1,32]{4,3,2,1,0:T(1,128)} %finish1.3.rest_0_), custom_call_target="tpu_custom_call", output_to_operand_aliasing={{}: (2, {})} | custom-call | tf_op jit(solution)/shard_map/finish2/pallas_call | solution.py:307
  88.5 0.0 collective-permute-done.1.src_ref
  88.5 0.0 copy-start.4
  88.6 0.7 copy-done.4
  89.2 2.4 %finish2.3 = f32[32,3,121,1,32]{4,3,2,1,0:T(1,128)} custom-call(s32[1]{0:T(128)S(6)} %rem.69.place_ref, f32[16,1,32,128]{3,2,1,0:T(8,128)} %copy-done.4, f32[32,3,121,1,32]{4,3,2,1,0:T(1,128)} %finish2.2.rest_0_), custom_call_target="tpu_custom_call", output_to_operand_aliasing={{}: (2, {})} | custom-call | tf_op jit(solution)/shard_map/finish2/pallas_call | solution.py:307
  (4 shorter events, 0.0 us)
Async XLA Ops:
  7.7 37.2 %copy-start.6 = (f32[11,11,1,32]{3,2,1,0:T(1,128)S(1)}, f32[11,11,1,32]{3,2,1,0:T(1,128)}, u32[]{:S(2)}) copy-start(f32[11,11,1,32]{3,2,1,0:T(1,128)} %param.13) | copy-start | bytes 46468
  7.7 37.3 %copy-start.7 = (f32[128]{0:T(128)S(1)}, f32[128]{0:T(128)}, u32[]{:S(2)}) copy-start(f32[128]{0:T(128)} %constant.90) | copy-start | bytes 1540
  7.7 41.5 %copy-start.8 = (f32[4,128]{1,0:T(4,128)S(1)}, f32[4,128]{1,0:T(4,128)}, u32[]{:S(2)}) copy-start(f32[4,128]{1,0:T(4,128)} %constant.81.clone) | copy-start | bytes 6148
  7.7 33.5 %all-to-all-start.1 = ((f32[32,2,2,16,128]{4,3,2,1,0:T(8,128)}), f32[32,2,2,16,128]{4,3,2,1,0:T(8,128)S(1)}, u32[]{:S(2)}, u32[]{:S(2)}) async-start(f32[32,2,2,16,128]{4,3,2,1,0:T(8,128)} %front0.1), calls=%async_computation.1 | async-start | bytes 2097152 | tf_op jit(solution)/shard_map/all_to_all | solution.py:407
  41.3 10.6 %copy-start = (f32[32,2,2,16,128]{4,3,2,1,0:T(8,128)}, f32[32,2,2,16,128]{4,3,2,1,0:T(8,128)S(1)}, u32[]{:S(2)}) copy-start(f32[32,2,2,16,128]{4,3,2,1,0:T(8,128)S(1)} %all-to-all-done.1) | copy-start | bytes 3145732
  41.3 24.9 %all-to-all-start = ((f32[32,1,2,16,128]{4,3,2,1,0:T(8,128)}), f32[32,1,2,16,128]{4,3,2,1,0:T(8,128)S(1)}, u32[]{:S(2)}, u32[]{:S(2)}) async-start(f32[32,1,2,16,128]{4,3,2,1,0:T(8,128)} %front2.1), calls=%async_computation | async-start | bytes 1048576 | tf_op jit(solution)/shard_map/all_to_all | solution.py:407
  45.0 4.2 %collective-permute-start = (f32[1,32,128]{2,1,0:T(8,128)S(1)}, f32[1,32,128]{2,1,0:T(8,128)S(1)}, u32[]{:S(2)}, u32[]{:S(2)}) collective-permute-start(f32[1,32,128]{2,1,0:T(8,128)S(1)} %get-tuple-element.17), channel_id=1, source_target_pairs={{0,1},{1,0},{2,3},{3,2},{4,5},{5,4},{6,7},{7,6},{8,9},{9,8},{10,11... | collective-permute-start | bytes 49160 | tf_op jit(solution)/shard_map/ppermute | solution.py:383
  49.2 0.6 copy-start.5
  58.0 19.3 %collective-permute-start.3 = (f32[16,1,32,128]{3,2,1,0:T(8,128)}, f32[16,1,32,128]{3,2,1,0:T(8,128)S(1)}, u32[]{:S(2)}, u32[]{:S(2)}) collective-permute-start(f32[16,1,32,128]{3,2,1,0:T(8,128)} %get-tuple-element.15), channel_id=1, source_target_pairs={{0,1},{1,0},{2,3},{3,2},{4,5},{5,4},{6,7},{7,6},{8,9},{9,8},{10,11... | collective-permute-start | bytes 786440 | tf_op jit(solution)/shard_map/ppermute | solution.py:417
  65.9 17.0 %collective-permute-start.2 = (f32[16,1,32,128]{3,2,1,0:T(8,128)}, f32[16,1,32,128]{3,2,1,0:T(8,128)S(1)}, u32[]{:S(2)}, u32[]{:S(2)}) collective-permute-start(f32[16,1,32,128]{3,2,1,0:T(8,128)} %get-tuple-element.13), channel_id=1, source_target_pairs={{0,1},{1,0},{2,3},{3,2},{4,5},{5,4},{6,7},{7,6},{8,9},{9,8},{10,11... | collective-permute-start | bytes 786440 | tf_op jit(solution)/shard_map/ppermute | solution.py:417
  66.2 0.8 copy-start.1
  73.1 15.5 %collective-permute-start.1 = (f32[16,1,32,128]{3,2,1,0:T(8,128)}, f32[16,1,32,128]{3,2,1,0:T(8,128)S(1)}, u32[]{:S(2)}, u32[]{:S(2)}) collective-permute-start(f32[16,1,32,128]{3,2,1,0:T(8,128)} %get-tuple-element.11), channel_id=1, source_target_pairs={{0,1},{1,0},{2,3},{3,2},{4,5},{5,4},{6,7},{7,6},{8,9},{9,8},{10,11... | collective-permute-start | bytes 786440 | tf_op jit(solution)/shard_map/ppermute | solution.py:417
  77.3 0.7 copy-start.3
  82.9 0.7 copy-start.2
  88.5 0.7 copy-start.4

commit v2 on v1

v2 whole, which is shorter than its diff:
```python
import functools
import math

import jax
import jax.numpy as jnp
import numpy as np
from jax import lax
from jax.experimental import pallas as pl
from jax.experimental.pallas import tpu as pltpu
from jax.sharding import PartitionSpec as P

MODES = 256
ITERS = 6
LANES = 128
GRANT = 16 << 20
CHUNKS = ((0, 1), (2,))

helm_base = 1.0
span_wave = 0.02
bound_ratio = 25.0


def legendre_pair(points, order):
    previous = points * 0.0 + 1.0
    current = points * 1.0
    for degree in range(2, order + 1):
        following = ((2 * degree - 1) * points * current - (degree - 1) * previous) / degree
        previous = current
        current = following
    return (current, previous)


def gll_tables(order):
    count = order + 1
    points = -np.cos(np.pi * np.arange(count) / order)
    for _ in range(200):
        top_vals, below_vals = legendre_pair(points, order)
        points = points - (points * top_vals - below_vals) / (count * top_vals)
    legendre_vals, below_vals = legendre_pair(points, order)
    weights = 2.0 / (order * (order + 1) * legendre_vals**2)
    identity = np.eye(count)
    spacing = points[:, None] - points[None, :] + identity
    derivative = legendre_vals[:, None] / (legendre_vals[None, :] * spacing) * (1.0 - identity)
    corner = np.concatenate(
        [[-order * (order + 1) / 4.0], np.zeros(order - 1), [order * (order + 1) / 4.0]]
    )
    derivative = derivative + identity * corner[None, :]
    stiffness = derivative.T @ (weights[:, None] * derivative)
    weight_mat = identity * weights[None, :]
    laplace = np.kron(stiffness, weight_mat) + np.kron(weight_mat, stiffness)
    lap_diag = np.diagonal(laplace)
    upper_bound = float(np.max(np.sum(np.abs(laplace), axis=1) / lap_diag))
    return (weights, derivative, laplace, lap_diag, upper_bound)


def split_table(table):
    table = np.asarray(table, np.float64)
    high = table.astype(jnp.bfloat16)
    low = (table - high.astype(np.float64)).astype(jnp.bfloat16)
    return (high, low)


def split_value(value):
    high = value.astype(jnp.bfloat16)
    low = (value - high.astype(jnp.float32)).astype(jnp.bfloat16)
    return (high, low)


def dft_tables(planes, kept, order):
    halves = len(order)
    first = np.arange(0, 2 * MODES, kept)
    tables = []
    for half in range(halves):
        row = (first[:, None] + np.array(order[half])[None, :]).reshape(-1)
        turns = np.arange(planes // halves)[None, :] * (row % MODES)[:, None] % planes
        angles = 2.0 * np.pi / planes * turns
        table = np.where((row < MODES)[:, None], np.cos(angles), -np.sin(angles))
        high, low = split_table(table / math.sqrt(planes))
        tables.append(np.concatenate([high, low], axis=1))
    return np.stack(tables)


def resident(value):
    return pltpu.with_memory_space_constraint(value, pltpu.VMEM)


def remote(value):
    return pltpu.with_memory_space_constraint(value, pltpu.HBM)


def padded(table, shape):
    result = np.zeros(shape, np.float64)
    result[tuple(slice(0, n) for n in table.shape)] = table
    return result


def dot(a, b, contract=((1,), (0,))):
    return lax.dot_general(a, b, (contract, ((), ())), preferred_element_type=jnp.float32)


def front_kernel(
    chunk, halves, local, field_ref, grad_ref, mass, dft_ref, out_ref, stage, grad, dft, ready, sems, out_sems
):
    comps, flat, lanes = field_ref.shape
    _, _, _, kept_all, rows = out_ref.shape
    kept = kept_all // halves
    planes = dft.shape[2] // 2 * halves
    pieces = planes // lanes
    nodes = flat // (pieces * local)
    order = [0, 1] + [c for c in chunk if c > 1]
    copies = {c: pltpu.make_async_copy(field_ref.at[c], stage.at[c], sems.at[c]) for c in order}
    grad_copy = pltpu.make_async_copy(grad_ref, grad, sems.at[comps])
    dft_copy = pltpu.make_async_copy(dft_ref, dft, sems.at[comps + 1])
    copies[0].start()
    grad_copy.start()
    for c in order[1:]:
        copies[c].start()
    dft_copy.start()
    gap = jnp.zeros((rows - nodes, planes), jnp.float32)

    def read(c, e):
        parts = [
            stage[c, pl.ds(piece * local + e, nodes, stride=pieces * local), :]
            for piece in range(pieces)
        ]
        return jnp.concatenate([jnp.concatenate(parts, axis=1), gap], axis=0)

    grad_copy.wait()
    copies[0].wait()
    copies[1].wait()
    for c in order[2:]:
        copies[c].wait()
    sent = []
    for slot, c in enumerate(chunk):
        for start in range(0, local, 2):
            elements = range(start, min(start + 2, local))
            folded = [[] for _ in range(halves)]
            for e in elements:
                value = read(c, e)
                high, low = split_value(value)
                slope = dot(grad[...], jnp.concatenate([high, low, high], axis=0))
                forcing = value - (read(0, e) * slope[:rows] + read(1, e) * slope[rows:])
                if halves == 2:
                    near, far = forcing[:, : planes // 2], forcing[:, planes // 2 :]
                    folded[0].append(near + far)
                    folded[1].append(near - far)
                else:
                    folded[0].append(forcing)
            if slot == 0 and start == 0:
                dft_copy.wait()
            for half in range(halves):
                high, low = split_value(jnp.concatenate(folded[half], axis=0))
                table = dft[half]
                spectra = dot(
                    jnp.concatenate([table[:, : planes // halves], table], axis=1),
                    jnp.concatenate([high, low, high], axis=1),
                    ((1,), (1,)),
                )
                for i, e in enumerate(elements):
                    part = spectra[:, i * rows : (i + 1) * rows] * mass[...]
                    ready[:, slot, e, half * kept : (half + 1) * kept, :] = part.reshape(
                        out_ref.shape[0], kept, rows
                    )
        copy = pltpu.make_async_copy(ready.at[:, slot], out_ref.at[:, slot], out_sems.at[slot])
        copy.start()
        sent.append(copy)
    for copy in sent:
        copy.wait()


def front(field, chunk, halves, local, tables, peers):
    grad, mass, dft = tables
    kept = dft.shape[0] * dft.shape[1] // peers
    far = pl.BlockSpec(memory_space=pltpu.HBM)
    shape = (peers, len(chunk), local, kept, LANES)
    return pl.pallas_call(
        functools.partial(front_kernel, chunk, halves, local),
        out_shape=pltpu.HBM(shape, jnp.float32),
        in_specs=[far, far, pl.BlockSpec(memory_space=pltpu.VMEM), far],
        out_specs=far,
        scratch_shapes=[
            pltpu.VMEM(field.shape, jnp.float32),
            pltpu.VMEM(grad.shape, grad.dtype),
            pltpu.VMEM(dft.shape, dft.dtype),
            pltpu.VMEM(shape, jnp.float32),
            pltpu.SemaphoreType.DMA((field.shape[0] + 2,)),
            pltpu.SemaphoreType.DMA((len(chunk),)),
        ],
        compiler_params=pltpu.CompilerParams(vmem_limit_bytes=GRANT),
    )(remote(field), remote(grad), mass, remote(dft))


def side_sum(value, before, after, masks):
    first, last = masks
    extra = 0.0
    if before is not None:
        extra = jnp.where(first, before, extra)
    if after is not None:
        extra = jnp.where(last, after, extra)
    return value if before is None and after is None else value + extra


def across(line, masks, side):
    result = []
    for col, value in enumerate(line):
        before = pltpu.roll(line[col - 1], LANES - side, 1) if col > 0 else None
        after = pltpu.roll(line[col + 1], side, 1) if col + 1 < len(line) else None
        result.append(side_sum(value, before, after, masks))
    return result


def read_masks(mask_ref, kept):
    bottom, top, left, right = (
        jnp.broadcast_to(mask_ref[i : i + 1, :], (kept, LANES)) > 0.5 for i in range(4)
    )
    return (bottom, top), (left, right)


def places(shape, kept):
    groups, owners, local_cols, local_rows = shape
    table = []
    for col in range(owners * local_cols):
        owner, lc = divmod(col, local_cols)
        line = []
        for row in range(groups * local_rows):
            part, e = divmod(row, local_rows)
            line.append((((part * owners + owner) * local_cols + lc) * local_rows + e) * kept)
        table.append(line)
    return table


def prep_kernel(shape, count, wave_ref, pen_ref, lap_ref, mask_ref, inverse_ref):
    kept = wave_ref.shape[0]
    along, over = read_masks(mask_ref, kept)
    where = places(shape, kept)
    cols, rows = len(where), len(where[0])
    base = wave_ref[...] + lap_ref[...]
    edge = pltpu.roll(base, count - 1, 1), pltpu.roll(base, LANES - count + 1, 1)
    for row in range(rows):
        line = []
        for col in range(cols):
            before = after = None
            if row > 0:
                other = pltpu.roll(pen_ref[col, row - 1 : row, :], LANES - count + 1, 1)
                before = edge[1] + other
            if row + 1 < rows:
                after = edge[0] + pltpu.roll(pen_ref[col, row + 1 : row + 2, :], count - 1, 1)
            line.append(side_sum(base + pen_ref[col, row : row + 1, :], before, after, along))
        for col, value in enumerate(across(line, over, (count - 1) * count)):
            first = where[col][row]
            inverse_ref[first : first + kept, :] = 1.0 / value


def solve_kernel(
    shape, midpoint, side, slot, span, gains, spot_ref, src_ref, inverse_ref, mat_ref, swap_ref, mask_ref, *rest
):
    groups, owners, local_cols, local_rows = shape
    outs = rest[:-5]
    work_ref, edge_ref, res_ref, dir_ref, sum_ref = rest[-5:]
    begin, end = span
    kept = end - begin
    along, over = read_masks(mask_ref, kept)
    where = places(shape, kept)
    whole = places(shape, src_ref.shape[-2])
    cols, rows_all = len(where), len(where[0])
    total = cols * rows_all * kept
    steps = math.gcd(groups, 4)
    block = total // steps
    parts = groups // steps

    def assembled(main, row):
        line = []
        for col in range(cols):
            before = after = None
            if row > 0:
                before = edge_ref[pl.ds(where[col][row - 1], kept), :]
            if row + 1 < rows_all:
                after = edge_ref[pl.ds(where[col][row + 1], kept), :]
            line.append(side_sum(main(col, row), before, after, along))
        return across(line, over, side)

    def source(col, row):
        owner, lc = divmod(col, local_cols)
        part, e = divmod(row, local_rows)
        return src_ref[part, owner, slot, lc * local_rows + e, begin:end]

    def inverse(col, row):
        return inverse_ref[pl.ds(whole[col][row] + begin, kept), :]

    def work(col, row):
        return work_ref[pl.ds(where[col][row], kept), :]

    for step in range(steps):
        values = src_ref[step * parts : (step + 1) * parts, :, slot, :, begin:end]
        values = values.reshape(block, LANES)
        high, low = split_value(values)
        edge_ref[pl.ds(step * block, block), :] = dot(
            jnp.concatenate([high, low], axis=1), swap_ref[...]
        )
    for row in range(rows_all):
        for col, value in enumerate(assembled(source, row)):
            here = pl.ds(where[col][row], kept)
            residual = inverse(col, row) * value
            direction = residual * (1.0 / midpoint)
            res_ref[here, :] = residual
            dir_ref[here, :] = direction
            sum_ref[pl.ds((col * rows_all + row) * kept, kept), :] = direction

    def sweep(step, carry):
        keep, gain = (jnp.float32(value) for value in gains[0])
        for i, (next_keep, next_gain) in enumerate(gains[1:]):
            keep = jnp.where(step > i, jnp.float32(next_keep), keep)
            gain = jnp.where(step > i, jnp.float32(next_gain), gain)

        def multiply(start):
            high, low = split_value(dir_ref[pl.ds(start, block), :])
            product = dot(jnp.concatenate([high, low, high], axis=1), mat_ref[...])
            work_ref[pl.ds(start, block), :] = product[:, :LANES]
            edge_ref[pl.ds(start, block), :] = product[:, LANES:]

        def update(row):
            for col, value in enumerate(assembled(work, row)):
                here = pl.ds(where[col][row], kept)
                direction = dir_ref[here, :]
                residual = res_ref[here, :] - direction - inverse(col, row) * value
                direction = keep * direction + gain * residual
                res_ref[here, :] = residual
                dir_ref[here, :] = direction
                there = pl.ds((col * rows_all + row) * kept, kept)
                sum_ref[there, :] = sum_ref[there, :] + direction

        done = 0
        multiply(0)
        for piece in range(1, steps + 1):
            if piece < steps:
                multiply(piece * block)
            ready = rows_all if piece == steps else piece * parts * local_rows - 1
            for row in range(done, ready):
                update(row)
            done = ready
        return carry

    lax.fori_loop(0, ITERS - 1, sweep, 0)

    spot = spot_ref[0]
    for shift, out in enumerate(outs):
        for lc in range(local_cols):
            col = lax.rem(spot + shift, owners) * local_cols + lc
            for k in range(kept):
                out[k, lc] = sum_ref[pl.ds(col * (rows_all * kept) + k, rows_all, stride=kept), :]


def solve(shape, midpoint, side, slot, span, spot, gains, moved, inverse, mat, swap, masks):
    groups, owners, local_cols, local_rows = shape
    kept = span[1] - span[0]
    rows = groups * local_rows
    total = owners * local_cols * rows * kept
    piece = pltpu.VMEM((kept, local_cols, rows, LANES), jnp.float32)
    smem = pl.BlockSpec(memory_space=pltpu.SMEM)
    vmem = pl.BlockSpec(memory_space=pltpu.VMEM)
    return pl.pallas_call(
        functools.partial(solve_kernel, shape, midpoint, side, slot, span, gains),
        out_shape=[piece] * owners,
        in_specs=[
            smem,
            vmem,
            vmem,
            vmem,
            vmem,
            vmem,
        ],
        out_specs=[vmem] * owners,
        scratch_shapes=[pltpu.VMEM((total, LANES), jnp.float32)] * 5,
        compiler_params=pltpu.CompilerParams(vmem_limit_bytes=GRANT),
    )(spot, *[resident(v) for v in (moved, inverse, mat, swap, masks)])


def finish_kernel(parts, owners, kept, order, spot_ref, *rest):
    sources = rest[: len(parts)]
    out_ref, stage_ref, sems = rest[-3:]
    nodes, local_cols, lanes = stage_ref.shape[1:]
    rows = sources[0].shape[2]
    fit = lanes // rows
    copies = []
    for source, (component, shift, begin) in zip(sources, parts):
        place = lax.rem(spot_ref[0] + (owners - shift), owners) * kept
        count = source.shape[0]
        for first in range(0, count, fit):
            group = range(first, min(first + fit, count))
            for lc in range(local_cols):
                block = [source[k, lc] for k in group]
                if len(group) * rows < lanes:
                    block.append(jnp.zeros((lanes - len(group) * rows, LANES), jnp.float32))
                turned = jnp.concatenate(block, axis=0).T
                for i, k in enumerate(group):
                    value = pltpu.roll(turned, lanes - i * rows, 1) if i else turned
                    stage_ref[len(copies) + i, :, lc, :] = value[:nodes]
            for k in group:
                target = out_ref.at[place + order[begin + k], component]
                index = len(copies)
                copy = pltpu.make_async_copy(stage_ref.at[index], target, sems.at[index])
                copy.start()
                copies.append(copy)
    for copy in copies:
        copy.wait()


def finish(parts, owners, kept, order, comps, nodes, spot, sources, so_far):
    _, local_cols, rows, _ = sources[0].shape
    width = pl.cdiv(rows, LANES) * LANES
    count = sum(source.shape[0] for source in sources)
    keep_out = pl.BlockSpec(memory_space=pl.ANY)
    in_specs = [pl.BlockSpec(memory_space=pltpu.SMEM)]
    in_specs += [pl.BlockSpec(memory_space=pltpu.VMEM)] * len(sources)
    args = [spot] + [resident(source) for source in sources]
    aliases = {}
    if so_far is not None:
        aliases = {len(args): 0}
        in_specs.append(keep_out)
        args.append(so_far)
    return pl.pallas_call(
        functools.partial(finish_kernel, parts, owners, kept, order),
        out_shape=jax.ShapeDtypeStruct((kept * owners, comps, nodes, local_cols, width), jnp.float32),
        in_specs=in_specs,
        out_specs=keep_out,
        scratch_shapes=[
            pltpu.VMEM((count, nodes, local_cols, width), jnp.float32),
            pltpu.SemaphoreType.DMA((count,)),
        ],
        input_output_aliases=aliases,
        compiler_params=pltpu.CompilerParams(vmem_limit_bytes=GRANT),
    )(*args)


def step(velocity, penalty):
    comps, count, _, local_cols, local_rows, planes = velocity.shape
    nodes = count * count
    groups = lax.axis_size("mode")
    owners = lax.axis_size("mesh")
    peers = groups * owners
    spot = lax.axis_index("mesh")
    local = local_cols * local_rows
    kept = 2 * MODES // peers
    total_cols = owners * local_cols
    total_rows = groups * local_rows

    weights, derivative, laplace, lap_diag, upper_bound = gll_tables(count - 1)
    mass = np.kron(weights, weights)
    lower_bound = upper_bound / bound_ratio
    midpoint = (upper_bound + lower_bound) / 2.0
    half_width = (upper_bound - lower_bound) / 2.0
    recurrence = half_width / midpoint
    gains = []
    for _ in range(1, ITERS):
        following = 1.0 / (2.0 * midpoint / half_width - recurrence)
        gains.append((following * recurrence, 2.0 * following / half_width))
        recurrence = following
    gains = tuple(gains)
    identity = np.eye(count)
    grads = np.concatenate(
        [
            padded(np.kron(derivative, identity), (LANES, LANES)),
            padded(np.kron(identity, derivative), (LANES, LANES)),
        ]
    )
    halves = 2 if kept % 16 == 0 else 1
    order = [list(range(half, kept, halves)) for half in range(halves)]
    flat_order = sum(order, [])
    grad_hi, grad_lo = split_table(grads)
    front_tables = [
        jnp.asarray(np.concatenate([grad_hi, grad_hi, grad_lo], axis=1)),
        jnp.asarray(padded(mass[None], (1, LANES)), jnp.float32),
        jnp.asarray(dft_tables(planes, kept, order)),
    ]

    off_diag = padded(laplace.T - np.diag(lap_diag), (LANES, LANES))
    swap = np.zeros((LANES, LANES))
    for a in range(count):
        swap[a * count, a * count + count - 1] = 1.0
        swap[a * count + count - 1, a * count] = 1.0
    shared = off_diag @ swap
    mat_hi, mat_lo = split_table(np.concatenate([off_diag, shared], axis=1))
    mat = jnp.asarray(np.concatenate([mat_hi, mat_hi, mat_lo], axis=0))
    swap = jnp.asarray(np.concatenate([swap, swap], axis=0), jnp.bfloat16)
    node = np.arange(LANES)
    real = node < nodes
    masks = np.stack(
        [
            real & (node % count == 0),
            real & (node % count == count - 1),
            real & (node // count == 0),
            real & (node // count == count - 1),
        ]
    ).astype(np.float32)
    masks = jnp.asarray(masks)
    lap_row = np.ones((1, LANES))
    lap_row[0, :nodes] = lap_diag
    lap_row = jnp.asarray(lap_row, jnp.float32)
    mass_row = jnp.asarray(padded(mass[None], (1, LANES)), jnp.float32)

    own = penalty.reshape(nodes, local_cols, total_rows).transpose(1, 2, 0)
    own = jnp.pad(own, ((0, 0), (0, 0), (0, LANES - nodes))) * mass_row
    full = jnp.zeros((total_cols, total_rows, LANES), jnp.float32)
    full = lax.dynamic_update_slice(full, own, (spot * local_cols, 0, 0))
    for shift in range(1, owners):
        ring = [(i, (i + shift) % owners) for i in range(owners)]
        other = lax.ppermute(own, "mesh", ring)
        full = lax.dynamic_update_slice(
            full, other, (lax.rem(spot + owners - shift, owners) * local_cols, 0, 0)
        )
    first_row = (lax.axis_index("mode") * owners + spot) * kept
    wave = ((first_row + jnp.asarray(flat_order, jnp.int32)) % MODES).astype(jnp.float32)
    helm = helm_base + (span_wave * wave) ** 2
    wave_mass = helm[:, None] * mass_row

    shape = (groups, owners, local_cols, local_rows)
    total = peers * local * kept
    inverse = pl.pallas_call(
        functools.partial(prep_kernel, shape, count),
        out_shape=pltpu.VMEM((total, LANES), jnp.float32),
        compiler_params=pltpu.CompilerParams(vmem_limit_bytes=GRANT),
        name="prep",
    )(*[resident(v) for v in (wave_mass, full, lap_row, masks)])

    field = velocity.reshape(comps, nodes, local, planes // LANES, LANES)
    field = field.transpose(0, 1, 3, 2, 4).reshape(comps, -1, LANES)

    spot_arg = spot.astype(jnp.int32)[None]
    pieces = {}
    for index, chunk in enumerate(CHUNKS):
        spectra = front(field, chunk, halves, local, front_tables, peers)
        if index:
            spectra, inverse = lax.optimization_barrier((spectra, inverse))
        moved = lax.all_to_all(spectra, ("mode", "mesh"), split_axis=0, concat_axis=0, tiled=True)
        moved = moved.reshape((groups, owners) + moved.shape[1:])
        for slot, component in enumerate(chunk):
            solved = solve(
                shape, midpoint, (count - 1) * count, slot, (0, kept),
                spot_arg, gains, moved, inverse, mat, swap, masks,
            )
            pieces[component, 0] = solved[0]
            for shift in range(1, owners):
                ring = [(i, (i + shift) % owners) for i in range(owners)]
                pieces[component, shift] = lax.ppermute(solved[shift], "mesh", ring)
    shifts = range(1, owners)
    groups_out = [
        [(0, 0), (1, 0)],
        [(2, 0)] + [(c, shift) for c in (0, 1) for shift in shifts],
        [(2, shift) for shift in shifts],
    ]
    result = None
    for group in groups_out:
        if group:
            result = finish(
                [(component, shift, 0) for component, shift in group], owners, kept, flat_order,
                comps, nodes, spot_arg, [pieces[key] for key in group], result,
            )
    result = result[..., :total_rows]
    return result.reshape(kept * owners, comps, count, count, local_cols, total_rows)


def solution(mesh):
    return jax.shard_map(
        step,
        mesh=mesh,
        in_specs=(P(None, None, None, "mesh", "mode", None), P(None, None, "mesh", None)),
        out_specs=P("mode", None, None, None, "mesh", None),
        check_vma=False,
    )
```

time: 92.4 us -> 72.3 us (0.78)
  Pallas kernels: 43.4 us -> 26.7 us
  local copies, waits for them, and re-layouts: 6.52 us -> 1.61 us
  other arithmetic: 0.69 us -> 2.07 us
    pallas_call x12 -> x9, Pallas kernels: 43.4 us -> 26.7 us  [the longest x3 10.3 us: solve(): pl.pallas_call(functools.partial(solve_kernel, shape, midpoint, side, slo...]
    unnamed x18 -> x10, local copies, waits for them, and re-layouts: 2.9 us -> 0.71 us
    pad x1 -> x0, local copies, waits for them, and re-layouts: 1.28 us -> none  [per_device(): jnp.pad(planes_first, ((0, 0), (0, 0), (0, LANES - nodes), (0, 0)))]
  transfers between devices with their start and end apart: 6 -> 6, of which waited for: 2 -> 3; matrix products, arithmetic and copies ran while one was open for 2% -> 4% of each run, Pallas kernels for 40% -> 30%
where the time goes in v2:
time: 72.3 us; the launch traced here: 71.8 us
  Pallas kernels  26.7 us (37%)
  waiting for transfers between devices  24.1 us (33%)
  starting transfers between devices  17 us (24%)
  other arithmetic  2.07 us (3%)
  local copies, waits for them, and re-layouts  1.61 us (2%)
    all_to_all x2, waiting for transfers between devices, step(): lax.all_to_all(spectra, ('mode', 'mesh'), split_axis=0, concat_axis=0, ti...  22.6 us
    all_to_all x2, starting transfers between devices, step(): lax.all_to_all(spectra, ('mode', 'mesh'), split_axis=0, concat_axis=0, ti...  11.2 us
    pallas_call x3, Pallas kernels, solve(): pl.pallas_call(functools.partial(solve_kernel, shape, midpoint, side, slo...  10.3 us
    pallas_call x3, Pallas kernels, finish(): pl.pallas_call(functools.partial(finish_kernel, parts, owners, kept, orde...  8.04 us
    pallas_call x2, Pallas kernels, front(): pl.pallas_call(functools.partial(front_kernel, chunk, halves, local), out...  7.09 us
    ppermute x3, starting transfers between devices, step(): pieces[component, shift] = lax.ppermute(solved[shift], 'mesh', ring)  4.1 us
    ppermute x1, starting transfers between devices, step(): other = lax.ppermute(own, 'mesh', ring)  1.77 us
    ppermute x3, waiting for transfers between devices, step(): pieces[component, shift] = lax.ppermute(solved[shift], 'mesh', ring)  1.5 us
  transfers between devices with their start and end apart: 6, of which 3 were waited for; matrix products, arithmetic and copies ran while one was open for 4% of the time, Pallas kernels for 30%

profile of v2, /device:TPU:0, one launch (start us, length us, event | category | flops | bytes accessed | tf_op | source)
XLA Modules:
  0.0 71.8 jit_solution(8892794921526386479)
XLA Ops:
  0.0 0.0 copy-start.2
  0.0 0.0 copy-start.4
  0.0 0.0 copy-start.1
  0.0 0.0 copy-start
  0.0 0.0 copy-start.3
  0.0 0.7 copy-done.3
  0.7 3.8 %shard_map.111 = f32[32,2,2,16,128]{4,3,2,1,0:T(8,128)} custom-call(f32[3,968,128]{2,1,0:T(8,128)} %bitcast.16, bf16[256,384]{1,0:T(8,128)(2,1)} %constant.57.clone.grad_ref, f32[1,128]{1,0:T(1,128)S(1)} %copy-done.3, bf16[2,256,512]{2,1,0:T(8,128)(2,1)} %constant.59.clone.dft_ref), custom_call_target="tpu_custom_call" | custom-call | tf_op jit(solution)/shard_map/pallas_call | solution.py:176
  4.5 7.4 %all-to-all-start.1 = ((f32[32,2,2,16,128]{4,3,2,1,0:T(8,128)}), f32[32,2,2,16,128]{4,3,2,1,0:T(8,128)S(1)}, u32[]{:S(2)}, u32[]{:S(2)}) async-start(f32[32,2,2,16,128]{4,3,2,1,0:T(8,128)} %shard_map.111), calls=%async_computation.1 | async-start | bytes 2097152 | tf_op jit(solution)/shard_map/all_to_all | solution.py:534
  11.9 0.9 %copy.17 = f32[121,1,32]{0,2,1:T(8,128)S(1)} copy(f32[121,1,32]{2,1,0:T(1,128)} %bitcast.19) | data formatting | bytes 30976 | tf_op jit(solution)/shard_map/reshape | solution.py:501
  12.8 0.7 pad_multiply_fusion
  13.5 1.8 %collective-permute-start = (f32[1,32,128]{2,1,0:T(8,128)S(1)}, f32[1,32,128]{2,1,0:T(8,128)S(1)}, u32[]{:S(2)}, u32[]{:S(2)}) collective-permute-start(f32[1,32,128]{2,1,0:T(8,128)S(1)} %get-tuple-element.21), channel_id=1, source_target_pairs={{0,1},{1,0},{2,3},{3,2},{4,5},{5,4},{6,7},{7,6},{8,9},{9,8},{10,11... | collective-permute-start | bytes 49160 | tf_op jit(solution)/shard_map/ppermute | solution.py:507
  15.2 0.7 fusion.4
  15.9 0.7 %broadcast_multiply_fusion.wave_ref = f32[16,128]{1,0:T(8,128)S(1)} fusion(f32[128]{0:T(128)} %constant.69, f32[16]{0:T(128)S(1)} %fusion.4), kind=kLoop, calls=%fused_computation.1 | loop fusion | flops 2048 | bytes 8768 | tf_op jit(solution)/shard_map/mul | solution.py:514
  16.6 3.3 %shard_map.109 = f32[32,1,2,16,128]{4,3,2,1,0:T(8,128)} custom-call(f32[3,968,128]{2,1,0:T(8,128)} %bitcast.17, bf16[256,384]{1,0:T(8,128)(2,1)} %constant.57.clone.grad_ref, f32[1,128]{1,0:T(1,128)S(1)} %copy-done.3, bf16[2,256,512]{2,1,0:T(8,128)(2,1)} %constant.59.clone.dft_ref), custom_call_target="tpu_custom_call" | custom-call | tf_op jit(solution)/shard_map/pallas_call | solution.py:176
  19.9 0.0 collective-permute-done
  20.0 0.0 copy-done.2
  20.0 0.0 copy-done.4
  20.0 1.3 %prep.1.inverse_ref = f32[1024,128]{1,0:T(8,128)S(1)} custom-call(f32[16,128]{1,0:T(8,128)S(1)} %broadcast_multiply_fusion.wave_ref, f32[2,32,128]{2,1,0:T(8,128)S(1)} %constant_dynamic-update-slice_fusion.pen_ref, f32[1,128]{1,0:T(1,128)S(1)} %copy-done.4, f32[4,128]{1,0:T(4,128)S(1)} %copy-done.2), custom_call_target="tpu_custom_call" | custom-call | tf_op jit(solution)/shard_map/prep/pallas_call | solution.py:518
  21.3 16.8 %all-to-all-done.1 = f32[32,2,2,16,128]{4,3,2,1,0:T(8,128)S(1)} async-done(((f32[32,2,2,16,128]{4,3,2,1,0:T(8,128)}), f32[32,2,2,16,128]{4,3,2,1,0:T(8,128)S(1)}, u32[]{:S(2)}, u32[]{:S(2)}) %all-to-all-start.1) | async-done | bytes 1048608 | tf_op jit(solution)/shard_map/all_to_all | solution.py:534
  38.1 3.8 %all-to-all-start = ((f32[32,1,2,16,128]{4,3,2,1,0:T(8,128)}), f32[32,1,2,16,128]{4,3,2,1,0:T(8,128)S(1)}, u32[]{:S(2)}, u32[]{:S(2)}) async-start(f32[32,1,2,16,128]{4,3,2,1,0:T(8,128)} %shard_map.109), calls=%async_computation | async-start | bytes 1048576 | tf_op jit(solution)/shard_map/all_to_all | solution.py:534
  41.9 0.0 copy-done.1
  41.9 0.0 copy-done
  41.9 3.4 %shard_map.113 = (f32[16,1,32,128]{3,2,1,0:T(8,128)S(1)}, f32[16,1,32,128]{3,2,1,0:T(8,128)S(1)}) custom-call(s32[1]{0:T(128)} %bitcast.spot_ref, f32[16,2,2,2,16,128]{5,4,3,2,1,0:T(8,128)S(1)} %bitcast.12, f32[1024,128]{1,0:T(8,128)S(1)} %prep.1.inverse_ref, bf16[384,256]{1,0:T(8,128)(2,1)S(1)} %copy-done, bf16[256,128]{1,0:T(8,128)(2,1)S(1)} %copy-done.1, ...), custom_call_target="tpu_custom_call" | custom-call | tf_op jit(solution)/shard_map/pallas_call | solution.py:361
  45.4 3.4 %shard_map.112 = (f32[16,1,32,128]{3,2,1,0:T(8,128)S(1)}, f32[16,1,32,128]{3,2,1,0:T(8,128)S(1)}) custom-call(s32[1]{0:T(128)} %bitcast.spot_ref, f32[16,2,2,2,16,128]{5,4,3,2,1,0:T(8,128)S(1)} %bitcast.13, f32[1024,128]{1,0:T(8,128)S(1)} %prep.1.inverse_ref, bf16[384,256]{1,0:T(8,128)(2,1)S(1)} %copy-done, bf16[256,128]{1,0:T(8,128)(2,1)S(1)} %copy-done.1, ...), custom_call_target="tpu_custom_call" | custom-call | tf_op jit(solution)/shard_map/pallas_call | solution.py:361
  48.8 1.7 %collective-permute-start.3 = (f32[16,1,32,128]{3,2,1,0:T(8,128)S(1)}, f32[16,1,32,128]{3,2,1,0:T(8,128)S(1)}, u32[]{:S(2)}, u32[]{:S(2)}) collective-permute-start(f32[16,1,32,128]{3,2,1,0:T(8,128)S(1)} %get-tuple-element.18), channel_id=1, source_target_pairs={{0,1},{1,0},{2,3},{3,2},{4,5},{5,4},{6,7},{7,6},{8,9},{9,8},{10,11... | collective-permute-start | bytes 786440 | tf_op jit(solution)/shard_map/ppermute | solution.py:544
  50.5 0.4 collective-permute-start.2
  50.9 5.8 %all-to-all-done = f32[32,1,2,16,128]{4,3,2,1,0:T(8,128)S(1)} async-done(((f32[32,1,2,16,128]{4,3,2,1,0:T(8,128)}), f32[32,1,2,16,128]{4,3,2,1,0:T(8,128)S(1)}, u32[]{:S(2)}, u32[]{:S(2)}) %all-to-all-start) | async-done | bytes 524320 | tf_op jit(solution)/shard_map/all_to_all | solution.py:534
  56.7 3.4 %shard_map.110 = (f32[16,1,32,128]{3,2,1,0:T(8,128)S(1)}, f32[16,1,32,128]{3,2,1,0:T(8,128)S(1)}) custom-call(s32[1]{0:T(128)} %bitcast.spot_ref, f32[16,2,1,2,16,128]{5,4,3,2,1,0:T(8,128)S(1)} %bitcast.14, f32[1024,128]{1,0:T(8,128)S(1)} %prep.1.inverse_ref, bf16[384,256]{1,0:T(8,128)(2,1)S(1)} %copy-done, bf16[256,128]{1,0:T(8,128)(2,1)S(1)} %copy-done.1, ...), custom_call_target="tpu_custom_call" | custom-call | tf_op jit(solution)/shard_map/pallas_call | solution.py:361
  60.1 2.0 %collective-permute-start.1 = (f32[16,1,32,128]{3,2,1,0:T(8,128)S(1)}, f32[16,1,32,128]{3,2,1,0:T(8,128)S(1)}, u32[]{:S(2)}, u32[]{:S(2)}) collective-permute-start(f32[16,1,32,128]{3,2,1,0:T(8,128)S(1)} %get-tuple-element.15), channel_id=1, source_target_pairs={{0,1},{1,0},{2,3},{3,2},{4,5},{5,4},{6,7},{7,6},{8,9},{9,8},{10,11... | collective-permute-start | bytes 786440 | tf_op jit(solution)/shard_map/ppermute | solution.py:544
  62.1 2.7 %shard_map.114.rest_3_ = f32[32,3,121,1,128]{4,3,2,1,0:T(1,128)} custom-call(s32[1]{0:T(128)} %bitcast.spot_ref, f32[16,1,32,128]{3,2,1,0:T(8,128)S(1)} %get-tuple-element.19.rest_0_, f32[16,1,32,128]{3,2,1,0:T(8,128)S(1)} %get-tuple-element.20.rest_1_), custom_call_target="tpu_custom_call" | custom-call | tf_op jit(solution)/shard_map/pallas_call | solution.py:421
  64.8 0.0 collective-permute-done.3.rest_2_
  64.8 0.0 collective-permute-done.2.rest_1_
  64.9 3.7 %shard_map.115.rest_1_ = f32[32,3,121,1,128]{4,3,2,1,0:T(1,128)} custom-call(s32[1]{0:T(128)} %bitcast.spot_ref, f32[16,1,32,128]{3,2,1,0:T(8,128)S(1)} %get-tuple-element.16.rest_0_, f32[16,1,32,128]{3,2,1,0:T(8,128)S(1)} %collective-permute-done.2.rest_1_, f32[16,1,32,128]{3,2,1,0:T(8,128)S(1)} %collective-permute-done.3.rest_2_, ...), custom_call_target="tpu_custom_call", output_to_operand_aliasing={{}: (4, {})} | custom-call | tf_op jit(solution)/shard_map/pallas_call | solution.py:421
  68.6 1.5 %collective-permute-done.1.rest_0_ = f32[16,1,32,128]{3,2,1,0:T(8,128)S(1)} collective-permute-done((f32[16,1,32,128]{3,2,1,0:T(8,128)S(1)}, f32[16,1,32,128]{3,2,1,0:T(8,128)S(1)}, u32[]{:S(2)}, u32[]{:S(2)}) %collective-permute-start.1) | collective-permute-done | bytes 262176 | tf_op jit(solution)/shard_map/ppermute | solution.py:544
  70.0 1.6 %shard_map.116 = f32[32,3,121,1,128]{4,3,2,1,0:T(1,128)} custom-call(s32[1]{0:T(128)} %bitcast.spot_ref, f32[16,1,32,128]{3,2,1,0:T(8,128)S(1)} %collective-permute-done.1.rest_0_, f32[32,3,121,1,128]{4,3,2,1,0:T(1,128)} %shard_map.115.rest_1_), custom_call_target="tpu_custom_call", output_to_operand_aliasing={{}: (2, {})} | custom-call | tf_op jit(solution)/shard_map/pallas_call | solution.py:421
  (2 shorter events, 0.0 us)
Async XLA Ops:
  0.0 20.0 %copy-start.2 = (f32[4,128]{1,0:T(4,128)S(1)}, f32[4,128]{1,0:T(4,128)}, u32[]{:S(2)}) copy-start(f32[4,128]{1,0:T(4,128)} %constant.62.clone.mask_ref) | copy-start | bytes 6148
  0.0 20.0 %copy-start.4 = (f32[1,128]{1,0:T(1,128)S(1)}, f32[1,128]{1,0:T(1,128)}, u32[]{:S(2)}) copy-start(f32[1,128]{1,0:T(1,128)} %constant.63.clone.lap_ref) | copy-start | bytes 1540
  0.0 41.9 %copy-start.1 = (bf16[256,128]{1,0:T(8,128)(2,1)S(1)}, bf16[256,128]{1,0:T(8,128)(2,1)}, u32[]{:S(2)}) copy-start(bf16[256,128]{1,0:T(8,128)(2,1)} %constant.61.clone.swap_ref) | copy-start | bytes 196612
  0.0 41.9 %copy-start = (bf16[384,256]{1,0:T(8,128)(2,1)S(1)}, bf16[384,256]{1,0:T(8,128)(2,1)}, u32[]{:S(2)}) copy-start(bf16[384,256]{1,0:T(8,128)(2,1)} %constant.60.clone.mat_ref) | copy-start | bytes 589828
  0.0 0.7 copy-start.3
  4.5 33.6 %all-to-all-start.1 = ((f32[32,2,2,16,128]{4,3,2,1,0:T(8,128)}), f32[32,2,2,16,128]{4,3,2,1,0:T(8,128)S(1)}, u32[]{:S(2)}, u32[]{:S(2)}) async-start(f32[32,2,2,16,128]{4,3,2,1,0:T(8,128)} %shard_map.111), calls=%async_computation.1 | async-start | bytes 2097152 | tf_op jit(solution)/shard_map/all_to_all | solution.py:534
  13.5 6.5 %collective-permute-start = (f32[1,32,128]{2,1,0:T(8,128)S(1)}, f32[1,32,128]{2,1,0:T(8,128)S(1)}, u32[]{:S(2)}, u32[]{:S(2)}) collective-permute-start(f32[1,32,128]{2,1,0:T(8,128)S(1)} %get-tuple-element.21), channel_id=1, source_target_pairs={{0,1},{1,0},{2,3},{3,2},{4,5},{5,4},{6,7},{7,6},{8,9},{9,8},{10,11... | collective-permute-start | bytes 49160 | tf_op jit(solution)/shard_map/ppermute | solution.py:507
  38.1 18.6 %all-to-all-start = ((f32[32,1,2,16,128]{4,3,2,1,0:T(8,128)}), f32[32,1,2,16,128]{4,3,2,1,0:T(8,128)S(1)}, u32[]{:S(2)}, u32[]{:S(2)}) async-start(f32[32,1,2,16,128]{4,3,2,1,0:T(8,128)} %shard_map.109), calls=%async_computation | async-start | bytes 1048576 | tf_op jit(solution)/shard_map/all_to_all | solution.py:534
  48.8 16.0 %collective-permute-start.3 = (f32[16,1,32,128]{3,2,1,0:T(8,128)S(1)}, f32[16,1,32,128]{3,2,1,0:T(8,128)S(1)}, u32[]{:S(2)}, u32[]{:S(2)}) collective-permute-start(f32[16,1,32,128]{3,2,1,0:T(8,128)S(1)} %get-tuple-element.18), channel_id=1, source_target_pairs={{0,1},{1,0},{2,3},{3,2},{4,5},{5,4},{6,7},{7,6},{8,9},{9,8},{10,11... | collective-permute-start | bytes 786440 | tf_op jit(solution)/shard_map/ppermute | solution.py:544
  50.5 14.4 %collective-permute-start.2 = (f32[16,1,32,128]{3,2,1,0:T(8,128)S(1)}, f32[16,1,32,128]{3,2,1,0:T(8,128)S(1)}, u32[]{:S(2)}, u32[]{:S(2)}) collective-permute-start(f32[16,1,32,128]{3,2,1,0:T(8,128)S(1)} %get-tuple-element.17), channel_id=1, source_target_pairs={{0,1},{1,0},{2,3},{3,2},{4,5},{5,4},{6,7},{7,6},{8,9},{9,8},{10,11... | collective-permute-start | bytes 786440 | tf_op jit(solution)/shard_map/ppermute | solution.py:544
  60.1 9.9 %collective-permute-start.1 = (f32[16,1,32,128]{3,2,1,0:T(8,128)S(1)}, f32[16,1,32,128]{3,2,1,0:T(8,128)S(1)}, u32[]{:S(2)}, u32[]{:S(2)}) collective-permute-start(f32[16,1,32,128]{3,2,1,0:T(8,128)S(1)} %get-tuple-element.15), channel_id=1, source_target_pairs={{0,1},{1,0},{2,3},{3,2},{4,5},{5,4},{6,7},{7,6},{8,9},{9,8},{10,11... | collective-permute-start | bytes 786440 | tf_op jit(solution)/shard_map/ppermute | solution.py:544
